TPU v7x, 512 devices: a whole 4x8x8 slice. The times are simulated.
512 devices in a mesh: grp: 64 (over x, z, core), tp: 8 (over y).
Axes of the slice: x: 4, y: 8, z: 8, core: 2. Of those that a mesh axis runs over, the one named last changes fastest.
Arguments:
- patches: bfloat16 [65536, 1280], P(('grp', 'tp')), may hold values from -6 to 6
- pictures: int32 [64, 1024], P('grp', 'tp'), may hold values from 0 to 1, as said below
- vis_qkv: bfloat16 [3, 1280, 1280], P(None, 'tp'), as said below
- vis_out: bfloat16 [1280, 1280], P(None, 'grp'), may hold values from -0.15625 to 0.15625
- merge_w: bfloat16 [1280, 5120], P('tp'), may hold values from -0.078125 to 0.078125
- text: bfloat16 [65536, 1280], P(('grp', 'tp')), may hold values from -6 to 6
- places: int32 [16384], P(('grp', 'tp')), may hold values from 0 to 65535, as said below
- segments: int32 [64, 1024], P('grp', 'tp'), may hold values from 0 to 3, never falling along the last dimension, each value on 1 to 512 neighbouring positions
- txt_qkv: bfloat16 [3, 1280, 1280], P(None, 'tp'), as said below
- txt_out: bfloat16 [1280, 1280], P(None, 'grp'), may hold values from -0.15625 to 0.15625
Outputs:
- hidden_out: bfloat16 [65536, 1280], P(('grp', 'tp'))
Inputs may be any that keep to these rules, and one draw needn't show every extreme that they name: `pictures`: within each row, picture numbers never fall; each picture is a run of whole aligned blocks of 4 positions and covers at least a quarter of the row, rounded down to whole blocks of 4 (at least one block). Row 0 holds one picture, row 1 two, the others one or two. `places`: all positions are distinct. The image rows of one device (aligned blocks of 32 rows, devices in the order of the placement) go to tokens held by the device of the same tp index in their token group: to 16 different token groups, exactly 2 rows to each. For each tp index, one token group receives 2 rows from every device of that tp index. `vis_qkv`: the query and key parts of a head may be correlated. `txt_qkv`: the query and key parts of a head may be correlated.
All inputs are finite; a program needn't handle non-finite values.
Results may differ from a plain program's by a relative error of at most 0.01.
Values may be sent and summed in bfloat16 or wider, within the bound.
A program may use at most 64 MiB of HBM per device.

v0:
```python
import jax
import jax.numpy as jnp
from jax import lax
from jax.sharding import PartitionSpec as P

HEAD_DIM = 80
SEND_CAP = 2


EPSILON = 1e-05
MASKED = -1e30


def layer_norm(rows):
    widened = rows.astype(jnp.float32)
    row_mean = jnp.mean(widened, axis=-1, keepdims=True)
    centred = widened - row_mean
    spread = jnp.mean(centred * centred, axis=-1, keepdims=True)
    return (centred * lax.rsqrt(spread + EPSILON)).astype(jnp.bfloat16)


def times_transpose(left, right):
    return lax.dot_general(
        left, right, (((1,), (1,)), ((), ())), preferred_element_type=jnp.float32
    )


def local_attention(queries, key_rows, value_rows, labels, causal):
    row_count, col_count = queries.shape
    heads_here = col_count // HEAD_DIM
    q_heads = queries.reshape(row_count, heads_here, HEAD_DIM)
    k_heads = key_rows.reshape(row_count, heads_here, HEAD_DIM)
    v_heads = value_rows.reshape(row_count, heads_here, HEAD_DIM)
    blocks = max(1, min(8, row_count // 512))
    block_rows = row_count // blocks
    inv_root = HEAD_DIM ** (-0.5)
    outputs = []
    for block_index in range(blocks):
        begin_row = block_index * block_rows
        end_key = begin_row + block_rows if causal else row_count
        scores = (
            jnp.einsum(
                "qhd,khd->hqk",
                q_heads[begin_row : begin_row + block_rows],
                k_heads[:end_key],
                preferred_element_type=jnp.float32,
            )
            * inv_root
        )
        allowed = labels[begin_row : begin_row + block_rows, None] == labels[None, :end_key]
        if causal:
            query_ids = jnp.arange(begin_row, begin_row + block_rows, dtype=jnp.int32)
            key_ids = jnp.arange(end_key, dtype=jnp.int32)
            allowed = allowed & (query_ids[:, None] >= key_ids[None, :])
        scores = jnp.where(allowed[None], scores, MASKED)
        row_max = jnp.max(scores, axis=-1, keepdims=True)
        weights = jnp.exp(scores - row_max)
        prob_bf = (weights / jnp.sum(weights, axis=-1, keepdims=True)).astype(jnp.bfloat16)
        mixed = jnp.einsum(
            "hqk,khd->qhd", prob_bf, v_heads[:end_key], preferred_element_type=jnp.float32
        )
        outputs.append(mixed.astype(jnp.bfloat16).reshape(block_rows, col_count))
    return jnp.concatenate(outputs, axis=0)


def attention_heads(gathered, weights, labels, causal):
    queries = times_transpose(gathered, weights[0]).astype(jnp.bfloat16)
    key_rows = times_transpose(gathered, weights[1]).astype(jnp.bfloat16)
    value_rows = times_transpose(gathered, weights[2]).astype(jnp.bfloat16)
    return local_attention(queries, key_rows, value_rows, labels, causal)


def project_out(rows_here, columns):
    return jnp.dot(
        rows_here,
        lax.all_gather(columns, "grp", axis=1, tiled=True),
        preferred_element_type=jnp.float32,
    )


def per_device(
    patches, pictures, vis_qkv, vis_out, merge_w, text, places, segments, txt_qkv, txt_out
):
    tp_count = lax.axis_size("tp")
    grp_count = lax.axis_size("grp")
    patch_normed = layer_norm(patches)
    group_rows, group_pics = (
        lax.all_gather(patch_normed, "tp", axis=0, tiled=True),
        lax.all_gather(pictures, "tp", axis=1, tiled=True),
    )
    heads_vis = attention_heads(group_rows, vis_qkv, group_pics[0], False)
    own_heads = lax.all_to_all(heads_vis, "tp", split_axis=0, concat_axis=1, tiled=True)
    vis_hidden = (patches.astype(jnp.float32) + project_out(own_heads, vis_out)).astype(
        jnp.bfloat16
    )
    merged = layer_norm(vis_hidden).reshape(patches.shape[0] // 4, 4 * patches.shape[1])
    image_cols = times_transpose(lax.all_gather(merged, "tp", axis=0, tiled=True), merge_w).astype(
        jnp.bfloat16
    )
    image_rows = lax.all_to_all(image_cols, "tp", split_axis=0, concat_axis=1, tiled=True)
    tok_count = text.shape[0]
    group_tokens = tok_count * tp_count
    dest_group = places // group_tokens
    dest_local = places % tok_count
    row_total = places.shape[0]
    row_ids = jnp.arange(row_total, dtype=jnp.int32)
    earlier = row_ids[:, None] > row_ids[None, :]
    same_dest = dest_group[:, None] == dest_group[None, :]
    slot_rank = jnp.sum((earlier & same_dest).astype(jnp.int32), axis=1)
    slot_index = dest_group * SEND_CAP + slot_rank
    slot_ids = jnp.arange(grp_count * SEND_CAP, dtype=jnp.int32)
    slot_pick = slot_ids[:, None] == slot_index[None, :]
    send_rows = jnp.dot(
        slot_pick.astype(jnp.bfloat16), image_rows, preferred_element_type=jnp.float32
    ).astype(jnp.bfloat16)
    send_pos = jnp.sum(jnp.where(slot_pick, dest_local[None, :] + 1, 0), axis=1) - 1
    send_rows = send_rows.reshape(grp_count, SEND_CAP, image_rows.shape[1])
    send_pos = send_pos.reshape(grp_count, SEND_CAP)
    recv_rows, recv_pos = (
        lax.all_to_all(send_rows, "grp", split_axis=0, concat_axis=0, tiled=True),
        lax.all_to_all(send_pos, "grp", split_axis=0, concat_axis=0, tiled=True),
    )
    recv_rows = recv_rows.reshape(grp_count * SEND_CAP, image_rows.shape[1])
    recv_pos = recv_pos.reshape(grp_count * SEND_CAP)
    position_hit = jnp.arange(tok_count, dtype=jnp.int32)[:, None] == recv_pos[None, :]
    placed = jnp.dot(
        position_hit.astype(jnp.bfloat16), recv_rows, preferred_element_type=jnp.float32
    ).astype(jnp.bfloat16)
    covered = jnp.any(position_hit, axis=1)
    prompt = jnp.where(covered[:, None], placed, text)
    token_normed = layer_norm(prompt)
    all_tokens, all_segments = (
        lax.all_gather(token_normed, "tp", axis=0, tiled=True),
        lax.all_gather(segments, "tp", axis=1, tiled=True),
    )
    heads_txt = attention_heads(all_tokens, txt_qkv, all_segments[0], True)
    own_text = lax.all_to_all(heads_txt, "tp", split_axis=0, concat_axis=1, tiled=True)
    return (prompt.astype(jnp.float32) + project_out(own_text, txt_out)).astype(jnp.bfloat16)


def solution(mesh):
    placed = (
        P(("grp", "tp"), None),
        P("grp", "tp"),
        P(None, "tp", None),
        P(None, "grp"),
        P("tp", None),
        P(("grp", "tp"), None),
        P(("grp", "tp")),
        P("grp", "tp"),
        P(None, "tp", None),
        P(None, "grp"),
    )
    return jax.shard_map(
        per_device, mesh=mesh, in_specs=placed, out_specs=P(("grp", "tp"), None), check_vma=False
    )
```

profile of v0, /device:TPU:56, one launch (start us, length us, event | category | flops | bytes accessed | tf_op | source)
XLA Modules:
  0.0 395.4 jit_solution(6746148892684774772)
XLA Ops:
  6.5 1.2 convert_reduce_fusion
  7.8 1.2 fusion.35
  9.0 1.9 fusion.36
  11.0 0.7 all-gather.14.cloned.1.call-update
  11.7 17.3 %all_gather.26 = s32[1,1024]{1,0:T(1,128)S(1)} all-gather(s32[1,128]{1,0:T(1,128)} %param.11), channel_id=1, replica_groups=mesh['grp'=64,'tp'=8] {'tp'}, dimensions={1}, use_global_device_ids=true | all-gather | bytes 4608 | tf_op jit(solution)/shard_map/all_gather | solution.py:89
  29.7 29.3 %all-gather.8.cloned.1.call-done = bf16[1024,1280]{1,0:T(8,128)(2,1)} async-done(((bf16[128,1280]{1,0:T(8,128)(2,1)}), bf16[1024,1280]{1,0:T(8,128)(2,1)}) %all-gather.8.cloned.1.call-update) | async-done | bytes 2621456 | tf_op jit(solution)/shard_map/all_gather | solution.py:88
  59.0 2.9 convolution_convert_fusion.6
  62.0 1.0 convolution_convert_fusion.7
  63.0 1.7 convolution_convert_fusion.5
  64.7 4.6 %fusion.79 = (f32[2,512]{1,0:T(2,128)S(1)}, f32[2,512,1024]{2,1,0:T(8,128)}) fusion(pred[512,1024]{1,0:T(8,128)(4,1)S(1)} %get-tuple-element.12, bf16[512,2,80]{0,2,1:T(8,128)(2,1)S(1)} %bitcast.111, bf16[1024,2,80]{0,2,1:T(8,128)(2,1)} %bitcast.132), kind=kOutput, calls=%fused_computation.131 | convolution fusion | flops 171967488 | bytes 5214208 | tf_op jit(solution)/shard_map/sub | solution.py:57
  69.3 4.6 %fusion.80 = (f32[2,512]{1,0:T(2,128)S(1)}, f32[2,512,1024]{2,1,0:T(8,128)}) fusion(pred[512,1024]{1,0:T(8,128)(4,1)S(1)} %get-tuple-element.11, bf16[512,2,80]{0,2,1:T(8,128)(2,1)S(1)} %bitcast.109, bf16[1024,2,80]{0,2,1:T(8,128)(2,1)} %bitcast.133), kind=kOutput, calls=%fused_computation.132 | convolution fusion | flops 171967488 | bytes 5214208 | tf_op jit(solution)/shard_map/sub | solution.py:57
  73.9 3.2 fusion.27
  77.4 0.8 fusion.28
  78.2 0.8 copy_bitcast_fusion.1
  79.0 5.3 %all-to-all-start.1 = ((bf16[8,128,160]{1,2,0:T(8,128)(2,1)}), bf16[8,128,160]{1,2,0:T(8,128)(2,1)S(1)}, u32[]{:S(2)}, u32[]{:S(2)}) async-start(bf16[8,128,160]{1,2,0:T(8,128)(2,1)} %copy_bitcast_fusion.1), calls=%async_computation.1 | async-start | bytes 655360 | tf_op jit(solution)/shard_map/all_to_all | solution.py:92
  84.4 62.2 %all-gather.14.cloned.1.call-done = bf16[64,20,1280]{2,1,0:T(8,128)(2,1)} async-done(((bf16[1,20,1280]{2,1,0:T(8,128)(2,1)}), bf16[64,20,1280]{2,1,0:T(8,128)(2,1)}) %all-gather.14.cloned.1.call-update) | async-done | bytes 3276816 | tf_op jit(solution)/shard_map/all_gather | solution.py:76
  146.5 6.1 %reshape.296 = bf16[1280,1280]{1,0:T(8,128)(2,1)} reshape(bf16[64,20,1280]{2,1,0:T(8,128)(2,1)} %all-gather.14.cloned.1.call-done) | data formatting | bytes 6553600
  152.7 3.2 fusion.81
  156.3 0.9 reshape.288
  157.6 40.5 %all-gather.10.cloned.1.call-done = bf16[256,5120]{1,0:T(8,128)(2,1)} async-done(((bf16[32,5120]{1,0:T(8,128)(2,1)}), bf16[256,5120]{1,0:T(8,128)(2,1)}) %all-gather.10.cloned.1.call-update) | async-done | bytes 2621456 | tf_op jit(solution)/shard_map/all_gather | solution.py:97
  198.1 2.8 convolution_convert_fusion.9
  200.9 0.8 copy.28
  201.6 5.4 %all-to-all-start.2 = ((bf16[8,32,160]{2,1,0:T(8,128)(2,1)}), bf16[8,32,160]{2,1,0:T(8,128)(2,1)S(1)}, u32[]{:S(2)}, u32[]{:S(2)}) async-start(bf16[8,32,160]{2,1,0:T(8,128)(2,1)} %bitcast.19), calls=%async_computation.2 | async-start | bytes 262144 | tf_op jit(solution)/shard_map/all_to_all | solution.py:100
  207.0 0.7 sub.70
  207.7 5.0 %all-to-all-done.2 = bf16[8,32,160]{2,1,0:T(8,128)(2,1)S(1)} async-done(((bf16[8,32,160]{2,1,0:T(8,128)(2,1)}), bf16[8,32,160]{2,1,0:T(8,128)(2,1)S(1)}, u32[]{:S(2)}, u32[]{:S(2)}) %all-to-all-start.2) | async-done | bytes 81952 | tf_op jit(solution)/shard_map/all_to_all | solution.py:100
  212.7 10.8 %all-to-all-start = ((s32[64,1,2]{2,1,0:T(1,128)}), s32[64,1,2]{2,1,0:T(1,128)S(1)}, u32[]{:S(2)}, u32[]{:S(2)}) async-start(s32[64,1,2]{2,1,0:T(1,128)} %bitcast), calls=%async_computation | async-start | bytes 65536 | tf_op jit(solution)/shard_map/all_to_all | solution.py:121
  224.1 0.8 reshape.289
  225.0 8.0 %all-to-all-done = s32[64,1,2]{2,1,0:T(1,128)S(1)} async-done(((s32[64,1,2]{2,1,0:T(1,128)}), s32[64,1,2]{2,1,0:T(1,128)S(1)}, u32[]{:S(2)}, u32[]{:S(2)}) %all-to-all-start) | async-done | bytes 544 | tf_op jit(solution)/shard_map/all_to_all | solution.py:121
  233.0 4.8 %all-to-all-start.3 = ((bf16[64,2,1280]{2,1,0:T(2,128)(2,1)}), bf16[64,2,1280]{2,1,0:T(2,128)(2,1)S(1)}, u32[]{:S(2)}, u32[]{:S(2)}) async-start(bf16[64,2,1280]{2,1,0:T(2,128)(2,1)} %reshape.289), calls=%async_computation.3 | async-start | bytes 655360 | tf_op jit(solution)/shard_map/all_to_all | solution.py:120
  238.5 0.8 reduce.3
  239.5 11.5 %all-to-all-done.3 = bf16[64,2,1280]{2,1,0:T(2,128)(2,1)S(1)} async-done(((bf16[64,2,1280]{2,1,0:T(2,128)(2,1)}), bf16[64,2,1280]{2,1,0:T(2,128)(2,1)S(1)}, u32[]{:S(2)}, u32[]{:S(2)}) %all-to-all-start.3) | async-done | bytes 327712 | tf_op jit(solution)/shard_map/all_to_all | solution.py:120
  251.7 0.9 multiply_convert_fusion
  253.2 15.6 %all_gather.31 = s32[1,1024]{1,0:T(1,128)S(1)} all-gather(s32[1,128]{1,0:T(1,128)S(1)} %copy-done.6), channel_id=1, replica_groups=mesh['grp'=64,'tp'=8] {'tp'}, dimensions={1}, use_global_device_ids=true | all-gather | bytes 4608 | tf_op jit(solution)/shard_map/all_gather | solution.py:134
  269.6 21.9 %all-gather.12.cloned.1.call-done = bf16[1024,1280]{1,0:T(8,128)(2,1)} async-done(((bf16[128,1280]{1,0:T(8,128)(2,1)}), bf16[1024,1280]{1,0:T(8,128)(2,1)}) %all-gather.12.cloned.1.call-update) | async-done | bytes 2621456 | tf_op jit(solution)/shard_map/all_gather | solution.py:133
  291.5 2.9 convolution_convert_fusion.4
  294.4 0.7 slice.97
  295.2 1.0 convolution_convert_fusion.2
  296.2 0.7 slice.100
  296.9 1.0 convolution_convert_fusion.3
  297.9 2.0 fusion.84
  299.9 2.3 convolution_convert_fusion.8
  302.3 4.6 %fusion.83 = (f32[2,512]{1,0:T(2,128)S(1)}, f32[2,512,1024]{2,1,0:T(8,128)}) fusion(pred[512,1024]{1,0:T(8,128)(4,1)S(1)} %fusion.18, bf16[512,2,80]{0,2,1:T(8,128)(2,1)S(1)} %bitcast.110, bf16[1024,2,80]{0,2,1:T(8,128)(2,1)} %bitcast.121), kind=kOutput, calls=%fused_computation.135 | convolution fusion | flops 171967488 | bytes 5214208 | tf_op jit(solution)/shard_map/sub | solution.py:57
  306.8 3.1 fusion.26
  310.0 0.8 copy_bitcast_fusion
  310.8 5.3 %all-to-all-start.4 = ((bf16[8,128,160]{1,2,0:T(8,128)(2,1)}), bf16[8,128,160]{1,2,0:T(8,128)(2,1)S(1)}, u32[]{:S(2)}, u32[]{:S(2)}) async-start(bf16[8,128,160]{1,2,0:T(8,128)(2,1)} %copy_bitcast_fusion), calls=%async_computation.4 | async-start | bytes 655360 | tf_op jit(solution)/shard_map/all_to_all | solution.py:137
  316.1 62.8 %all-gather.16.cloned.1.call-done = bf16[64,20,1280]{2,1,0:T(8,128)(2,1)} async-done(((bf16[1,20,1280]{2,1,0:T(8,128)(2,1)}), bf16[64,20,1280]{2,1,0:T(8,128)(2,1)}) %all-gather.16.cloned.1.call-update) | async-done | bytes 3276816 | tf_op jit(solution)/shard_map/all_gather | solution.py:76
  378.9 6.1 %reshape.298 = bf16[1280,1280]{1,0:T(8,128)(2,1)} reshape(bf16[64,20,1280]{2,1,0:T(8,128)(2,1)} %all-gather.16.cloned.1.call-done) | data formatting | bytes 6553600
  385.0 3.9 fusion.8
  (67 shorter events, 5.4 us)
Async XLA Ops:
  6.5 191.6 %copy-start = (bf16[160,5120]{1,0:T(8,128)(2,1)S(1)}, bf16[160,5120]{1,0:T(8,128)(2,1)}, u32[]{:S(2)}) copy-start(bf16[160,5120]{1,0:T(8,128)(2,1)} %param.14) | copy-start | bytes 4915204
  6.5 52.4 %all-gather.8.cloned.1.call-start = ((), (), s32[]{:S(2)}) async-start(), calls=%async_computation.5 | async-start | bytes 2949120 | tf_op jit(solution)/shard_map/all_gather | solution.py:88
  10.9 135.6 %all-gather.14.cloned.1.call-start = ((), (), s32[]{:S(2)}) async-start(), calls=%async_computation.8 | async-start | bytes 3993600 | tf_op jit(solution)/shard_map/all_gather | solution.py:76
  59.0 3.0 copy-start.7
  59.0 3.0 copy-start.9
  73.9 3.5 copy-start.12
  79.0 73.6 %all-to-all-start.1 = ((bf16[8,128,160]{1,2,0:T(8,128)(2,1)}), bf16[8,128,160]{1,2,0:T(8,128)(2,1)S(1)}, u32[]{:S(2)}, u32[]{:S(2)}) async-start(bf16[8,128,160]{1,2,0:T(8,128)(2,1)} %copy_bitcast_fusion.1), calls=%async_computation.1 | async-start | bytes 655360 | tf_op jit(solution)/shard_map/all_to_all | solution.py:92
  84.4 68.3 %copy-start.1 = (bf16[128,1280]{1,0:T(8,128)(2,1)S(1)}, bf16[128,1280]{1,0:T(8,128)(2,1)}, u32[]{:S(2)}) copy-start(bf16[128,1280]{1,0:T(8,128)(2,1)} %param.10) | copy-start | bytes 983044
  84.4 113.7 %all-gather.10.cloned.1.call-start = ((), (), s32[]{:S(2)}) async-start(), calls=%async_computation.6 | async-start | bytes 2949120 | tf_op jit(solution)/shard_map/all_gather | solution.py:97
  152.7 4.6 %copy-start.11 = (s32[32]{0:T(128)S(1)}, s32[32]{0:T(128)}, u32[]{:S(2)}) copy-start(s32[32]{0:T(128)} %param.16) | copy-start | bytes 388
  200.9 50.3 %copy-start.2 = (bf16[128,1280]{1,0:T(8,128)(2,1)S(1)}, bf16[128,1280]{1,0:T(8,128)(2,1)}, u32[]{:S(2)}) copy-start(bf16[128,1280]{1,0:T(8,128)(2,1)} %param.15) | copy-start | bytes 983044
  201.6 11.1 %all-to-all-start.2 = ((bf16[8,32,160]{2,1,0:T(8,128)(2,1)}), bf16[8,32,160]{2,1,0:T(8,128)(2,1)S(1)}, u32[]{:S(2)}, u32[]{:S(2)}) async-start(bf16[8,32,160]{2,1,0:T(8,128)(2,1)} %bitcast.19), calls=%async_computation.2 | async-start | bytes 262144 | tf_op jit(solution)/shard_map/all_to_all | solution.py:100
  212.7 20.3 %all-to-all-start = ((s32[64,1,2]{2,1,0:T(1,128)}), s32[64,1,2]{2,1,0:T(1,128)S(1)}, u32[]{:S(2)}, u32[]{:S(2)}) async-start(s32[64,1,2]{2,1,0:T(1,128)} %bitcast), calls=%async_computation | async-start | bytes 65536 | tf_op jit(solution)/shard_map/all_to_all | solution.py:121
  224.1 29.1 %copy-start.6 = (s32[1,128]{1,0:T(1,128)S(1)}, s32[1,128]{1,0:T(1,128)}, u32[]{:S(2)}) copy-start(s32[1,128]{1,0:T(1,128)} %param.17) | copy-start | bytes 1540
  233.0 18.0 %all-to-all-start.3 = ((bf16[64,2,1280]{2,1,0:T(2,128)(2,1)}), bf16[64,2,1280]{2,1,0:T(2,128)(2,1)S(1)}, u32[]{:S(2)}, u32[]{:S(2)}) async-start(bf16[64,2,1280]{2,1,0:T(2,128)(2,1)} %reshape.289), calls=%async_computation.3 | async-start | bytes 655360 | tf_op jit(solution)/shard_map/all_to_all | solution.py:120
  237.8 53.6 %all-gather.12.cloned.1.call-start = ((), (), s32[]{:S(2)}) async-start(), calls=%async_computation.7 | async-start | bytes 2949120 | tf_op jit(solution)/shard_map/all_gather | solution.py:133
  252.6 126.2 %all-gather.16.cloned.1.call-start = ((), (), s32[]{:S(2)}) async-start(), calls=%async_computation.9 | async-start | bytes 3993600 | tf_op jit(solution)/shard_map/all_gather | solution.py:76
  291.5 3.7 copy-start.8
  291.5 3.7 copy-start.10
  294.4 1.7 copy-start.4
  296.2 1.7 copy-start.5
  297.9 2.0 copy-start.3
  310.8 74.2 %all-to-all-start.4 = ((bf16[8,128,160]{1,2,0:T(8,128)(2,1)}), bf16[8,128,160]{1,2,0:T(8,128)(2,1)S(1)}, u32[]{:S(2)}, u32[]{:S(2)}) async-start(bf16[8,128,160]{1,2,0:T(8,128)(2,1)} %copy_bitcast_fusion), calls=%async_computation.4 | async-start | bytes 655360 | tf_op jit(solution)/shard_map/all_to_all | solution.py:137
Sparse Core Ops, SparseCore 0:
  11.0 47.8 all-gather.7
  62.2 84.2 all-gather.13
  157.4 40.6 all-gather.9
  252.8 38.6 all-gather.11
  294.6 84.2 all-gather.15
where the time goes:
time: 398 us; the launch traced here: 395 us
  waiting for transfers between devices  242 us (61%)
  matrix products  46.3 us (12%)
  blocking collectives  32.9 us (8%)
  starting transfers between devices  31.8 us (8%)
  local copies, waits for them, and re-layouts  18.5 us (5%)
  between operations  13.5 us (3%)
  other arithmetic  10 us (3%)
    all_gather x2, waiting for transfers between devices, project_out(): lax.all_gather(columns, 'grp', axis=1, tiled=True)  125 us
    all_gather x1, waiting for transfers between devices, per_device(): lax.all_gather(merged, 'tp', axis=0, tiled=True)  40.5 us
    all_gather x1, waiting for transfers between devices, per_device(): lax.all_gather(patch_normed, 'tp', axis=0, tiled=True)  29.3 us
    all_gather x1, waiting for transfers between devices, per_device(): lax.all_gather(token_normed, 'tp', axis=0, tiled=True)  21.9 us
    all_gather x1, blocking collectives, per_device(): lax.all_gather(pictures, 'tp', axis=1, tiled=True)  17.3 us
    sub x4, matrix products, local_attention(): weights = jnp.exp(scores - row_max)  15.8 us
    all_gather x1, blocking collectives, per_device(): lax.all_gather(segments, 'tp', axis=1, tiled=True)  15.6 us
    dot_general x7, matrix products, times_transpose(): lax.dot_general(left, right, (((1,), (1,)), ((), ())), preferred_element_...  13.3 us
  transfers between devices with their start and end apart: 10, of which 8 were waited for; matrix products, arithmetic and copies ran while one was open for 14% of the time, Pallas kernels for 0%

commit v1 on v0

--- a/solution.py
+++ b/solution.py
@@ -1,14 +1,25 @@
+import functools
+
 import jax
 import jax.numpy as jnp
 from jax import lax
+from jax.experimental import pallas as pl
+from jax.experimental.pallas import tpu as pltpu
 from jax.sharding import PartitionSpec as P
 
 HEAD_DIM = 80
 SEND_CAP = 2
+N_TP = 8
+N_Z = 8
+N_X = 4
+SHARD = 20
+SHARD_PAD = 24
+LANES = 128
 
 
 EPSILON = 1e-05
 MASKED = -1e30
+MESH = pl.DeviceIdType.MESH
 
 
 def layer_norm(rows):
@@ -23,6 +34,232 @@
     return lax.dot_general(
         left, right, (((1,), (1,)), ((), ())), preferred_element_type=jnp.float32
     )
+
+
+def wrap(value, count):
+    return lax.rem(value + count, count)
+
+
+def greet(devices):
+    barrier = pltpu.get_barrier_semaphore()
+    for device in devices:
+        pl.semaphore_signal(barrier, inc=1, device_id=device, device_id_type=MESH)
+    pl.semaphore_wait(barrier, len(devices))
+
+
+def gather_kernel(with_extras, *refs):
+    if with_extras:
+        own, own_label, own_shard, rows, labels, shards, *sems = refs
+        row_send, row_recv, local_sem, lab_send, lab_recv, z_send, z_recv, x_send, x_recv = sems
+    else:
+        own, rows, row_send, row_recv, local_sem = refs
+    tp = lax.axis_index("tp")
+    grp = lax.axis_index("grp")
+    core = lax.rem(grp, 2)
+    z_here = lax.rem(grp // 2, N_Z)
+    x_here = grp // (2 * N_Z)
+    half = own.shape[0] // 2
+
+    def at_xz(x, z):
+        return {"grp": (x * N_Z + z) * 2 + core}
+
+    def remote(src, dst, send, recv, device):
+        return pltpu.make_async_remote_copy(
+            src_ref=src,
+            dst_ref=dst,
+            send_sem=send,
+            recv_sem=recv,
+            device_id=device,
+            device_id_type=MESH,
+        )
+
+    neighbours = [{"tp": wrap(tp + 1, N_TP)}, {"tp": wrap(tp - 1, N_TP)}]
+    if with_extras:
+        z_next = [at_xz(x_here, wrap(z_here + 1, N_Z)), at_xz(x_here, wrap(z_here - 1, N_Z))]
+        x_peers = [at_xz(wrap(x_here + d, N_X), z_here) for d in range(1, N_X)]
+        greet(neighbours + z_next + x_peers)
+    else:
+        greet(neighbours)
+
+    def row_copy(way, step, part):
+        block = wrap(tp - step, N_TP) if way == 0 else wrap(tp + step, N_TP)
+        span = pl.ds(part * half, half)
+        dst = rows.at[block, span]
+        src = own.at[span] if step == 0 else dst
+        slot = (way * 4 + step) * 2 + part
+        return remote(src, dst, row_send.at[slot], row_recv.at[slot], neighbours[way])
+
+    def label_copy(way, step):
+        block = wrap(tp - step, N_TP) if way == 0 else wrap(tp + step, N_TP)
+        dst = labels.at[block]
+        src = own_label if step == 0 else dst
+        slot = way * 4 + step
+        return remote(src, dst, lab_send.at[slot], lab_recv.at[slot], neighbours[way])
+
+    def shard_copy(way, step, part):
+        block = wrap(z_here - step, N_Z) if way == 0 else wrap(z_here + step, N_Z)
+        piece = shards.at[block, pl.ds(part * 2, 2)]
+        slot = (way * 4 + step) * 2 + part
+        return remote(piece, piece, z_send.at[slot], z_recv.at[slot], z_next[way])
+
+    local = [pltpu.make_async_copy(own, rows.at[tp], local_sem.at[0])]
+    if with_extras:
+        local.append(pltpu.make_async_copy(own_label, labels.at[tp], local_sem.at[1]))
+        own_place = shards.at[z_here, x_here]
+        local.append(pltpu.make_async_copy(own_shard, own_place, local_sem.at[2]))
+    for copy in local:
+        copy.start()
+    pending = []
+
+    def start(copy):
+        copy.start()
+        pending.append(copy)
+
+    if with_extras:
+        x_copies = [
+            remote(own_shard, own_place, x_send.at[d], x_recv.at[d], x_peers[d])
+            for d in range(N_X - 1)
+        ]
+        for copy in x_copies:
+            start(copy)
+    row_ring = {}
+    for part in range(2):
+        for way in range(2):
+            row_ring[way, 0, part] = row_copy(way, 0, part)
+            start(row_ring[way, 0, part])
+    if with_extras:
+        label_ring = {(way, 0): label_copy(way, 0) for way in range(2)}
+        for way in range(2):
+            start(label_ring[way, 0])
+    for copy in local:
+        copy.wait()
+    if with_extras:
+        for copy in x_copies:
+            copy.wait_recv()
+        shard_ring = {}
+        for part in range(2):
+            for way in range(2):
+                shard_ring[way, 0, part] = shard_copy(way, 0, part)
+                start(shard_ring[way, 0, part])
+    for step in range(1, 4):
+        for part in range(2):
+            for way in range(2):
+                row_ring[way, step - 1, part].wait_recv()
+                if step < 3 or part == way:
+                    row_ring[way, step, part] = row_copy(way, step, part)
+                    start(row_ring[way, step, part])
+            if with_extras:
+                for way in range(2):
+                    shard_ring[way, step - 1, part].wait_recv()
+                    if step < 3 or part == way:
+                        shard_ring[way, step, part] = shard_copy(way, step, part)
+                        start(shard_ring[way, step, part])
+        if with_extras:
+            for way in range(2):
+                label_ring[way, step - 1].wait_recv()
+                if step < 3 or way == 0:
+                    label_ring[way, step] = label_copy(way, step)
+                    start(label_ring[way, step])
+    for way in range(2):
+        row_ring[way, 3, way].wait_recv()
+        if with_extras:
+            shard_ring[way, 3, way].wait_recv()
+    if with_extras:
+        label_ring[0, 3].wait_recv()
+    for copy in pending:
+        copy.wait_send()
+
+
+def gather_rows(own, collective_id, own_label=None, own_shard=None):
+    with_extras = own_label is not None
+    vmem = pl.BlockSpec(memory_space=pltpu.VMEM)
+    hbm = pl.BlockSpec(memory_space=pl.ANY)
+    operands = [own]
+    shapes = [jax.ShapeDtypeStruct((N_TP, *own.shape), own.dtype)]
+    dma = pltpu.SemaphoreType.DMA
+    scratch = [dma((16,)), dma((16,)), dma((3,))]
+    if with_extras:
+        operands += [own_label, own_shard]
+        shapes.append(jax.ShapeDtypeStruct((N_TP, *own_label.shape), own_label.dtype))
+        shapes.append(jax.ShapeDtypeStruct((N_Z, N_X, *own_shard.shape), own_shard.dtype))
+        scratch += [dma((8,)), dma((8,)), dma((16,)), dma((16,)), dma((3,)), dma((3,))]
+    return pl.pallas_call(
+        functools.partial(gather_kernel, with_extras),
+        out_shape=shapes,
+        in_specs=[vmem] * len(operands),
+        out_specs=[hbm] * len(shapes),
+        scratch_shapes=scratch,
+        compiler_params=pltpu.CompilerParams(collective_id=collective_id, has_side_effects=True),
+    )(*operands)
+
+
+PIECES = 4
+
+
+def swap_kernel(with_shards, *refs):
+    if with_shards:
+        blocks, shards, received, other, send, recv, local_sem, core_send, core_recv = refs
+    else:
+        blocks, received, send, recv, local_sem = refs
+    tp = lax.axis_index("tp")
+    grp = lax.axis_index("grp")
+    partner = {"grp": grp + 1 - 2 * lax.rem(grp, 2)}
+    peers = [{"tp": wrap(tp + d, N_TP)} for d in range(1, N_TP)]
+    greet(peers + [partner] if with_shards else peers)
+    own = pltpu.make_async_copy(blocks.at[tp], received.at[tp], local_sem)
+    own.start()
+    copies = []
+    for d in (4, 3, 5, 2, 6, 1, 7):
+        copies.append(
+            pltpu.make_async_remote_copy(
+                src_ref=blocks.at[wrap(tp + d, N_TP)],
+                dst_ref=received.at[tp],
+                send_sem=send.at[d],
+                recv_sem=recv.at[d],
+                device_id=peers[d - 1],
+                device_id_type=MESH,
+            )
+        )
+    if with_shards:
+        count = shards.shape[0] // PIECES
+        for piece in range(PIECES):
+            span = pl.ds(piece * count, count)
+            copies.append(
+                pltpu.make_async_remote_copy(
+                    src_ref=shards.at[span],
+                    dst_ref=other.at[span],
+                    send_sem=core_send.at[piece],
+                    recv_sem=core_recv.at[piece],
+                    device_id=partner,
+                    device_id_type=MESH,
+                )
+            )
+    for copy in copies:
+        copy.start()
+    own.wait()
+    for copy in copies:
+        copy.wait()
+
+
+def swap_blocks(blocks, collective_id, shards=None):
+    with_shards = shards is not None
+    vmem = pl.BlockSpec(memory_space=pltpu.VMEM)
+    hbm = pl.BlockSpec(memory_space=pl.ANY)
+    dma = pltpu.SemaphoreType.DMA
+    scratch = [dma((N_TP,)), dma((N_TP,)), dma]
+    operands, specs = [blocks], [vmem]
+    if with_shards:
+        operands.append(shards)
+        specs.append(hbm)
+        scratch += [dma((PIECES,)), dma((PIECES,))]
+    return pl.pallas_call(
+        functools.partial(swap_kernel, with_shards),
+        out_shape=[jax.ShapeDtypeStruct(a.shape, a.dtype) for a in operands],
+        in_specs=specs,
+        out_specs=[hbm] * len(operands),
+        scratch_shapes=scratch,
+        compiler_params=pltpu.CompilerParams(collective_id=collective_id, has_side_effects=True),
+    )(*operands)
 
 
 def local_attention(queries, key_rows, value_rows, labels, causal):
@@ -70,12 +307,27 @@
     return local_attention(queries, key_rows, value_rows, labels, causal)
 
 
-def project_out(rows_here, columns):
-    return jnp.dot(
-        rows_here,
-        lax.all_gather(columns, "grp", axis=1, tiled=True),
-        preferred_element_type=jnp.float32,
+def attention_layer(rows, labels, qkv, columns, causal, first_id):
+    shard = jnp.pad(columns.T, ((0, SHARD_PAD - SHARD), (0, 0)))
+    gathered, all_labels, shards = gather_rows(layer_norm(rows), first_id, labels, shard)
+    row_total = N_TP * rows.shape[0]
+    heads = attention_heads(
+        gathered.reshape(row_total, rows.shape[1]), qkv, all_labels.reshape(row_total), causal
     )
+    blocks = heads.reshape(N_TP, rows.shape[0], heads.shape[1]).transpose(0, 2, 1)
+    own_heads, other = swap_blocks(blocks, first_id + 1, shards)
+    own_heads = own_heads.reshape(rows.shape[1], rows.shape[0])
+
+    def project(part):
+        flat = part.reshape(N_Z * N_X * SHARD_PAD, rows.shape[1])
+        return jnp.dot(flat, own_heads, preferred_element_type=jnp.float32)
+
+    here, there = project(shards), project(other)
+    first = lax.rem(lax.axis_index("grp"), 2) == 0
+    both = jnp.stack([jnp.where(first, here, there), jnp.where(first, there, here)])
+    both = both.reshape(2, N_Z, N_X, SHARD_PAD, rows.shape[0])[:, :, :, :SHARD]
+    projected = both.transpose(4, 2, 1, 0, 3).reshape(rows.shape)
+    return (rows.astype(jnp.float32) + projected).astype(jnp.bfloat16)
 
 
 def per_device(
@@ -83,59 +335,45 @@
 ):
     tp_count = lax.axis_size("tp")
     grp_count = lax.axis_size("grp")
-    patch_normed = layer_norm(patches)
-    group_rows, group_pics = (
-        lax.all_gather(patch_normed, "tp", axis=0, tiled=True),
-        lax.all_gather(pictures, "tp", axis=1, tiled=True),
-    )
-    heads_vis = attention_heads(group_rows, vis_qkv, group_pics[0], False)
-    own_heads = lax.all_to_all(heads_vis, "tp", split_axis=0, concat_axis=1, tiled=True)
-    vis_hidden = (patches.astype(jnp.float32) + project_out(own_heads, vis_out)).astype(
-        jnp.bfloat16
-    )
-    merged = layer_norm(vis_hidden).reshape(patches.shape[0] // 4, 4 * patches.shape[1])
-    image_cols = times_transpose(lax.all_gather(merged, "tp", axis=0, tiled=True), merge_w).astype(
-        jnp.bfloat16
-    )
-    image_rows = lax.all_to_all(image_cols, "tp", split_axis=0, concat_axis=1, tiled=True)
+    width = patches.shape[1]
+    vis_hidden = attention_layer(patches, pictures, vis_qkv, vis_out, False, 0)
+    merged = layer_norm(vis_hidden).reshape(patches.shape[0] // 4, 4 * width)
+    (all_merged,) = gather_rows(merged, 2)
+    row_total = places.shape[0]
+    image_cols = times_transpose(
+        all_merged.reshape(tp_count * row_total, 4 * width), merge_w
+    ).astype(jnp.bfloat16)
+    (image_parts,) = swap_blocks(image_cols.reshape(tp_count, row_total, -1), 3)
+    image_rows = image_parts.transpose(1, 0, 2).reshape(row_total, width)
     tok_count = text.shape[0]
     group_tokens = tok_count * tp_count
     dest_group = places // group_tokens
     dest_local = places % tok_count
-    row_total = places.shape[0]
     row_ids = jnp.arange(row_total, dtype=jnp.int32)
     earlier = row_ids[:, None] > row_ids[None, :]
     same_dest = dest_group[:, None] == dest_group[None, :]
     slot_rank = jnp.sum((earlier & same_dest).astype(jnp.int32), axis=1)
     slot_index = dest_group * SEND_CAP + slot_rank
     slot_ids = jnp.arange(grp_count * SEND_CAP, dtype=jnp.int32)
-    slot_pick = slot_ids[:, None] == slot_index[None, :]
+    slot_pick = (slot_ids[:, None] == slot_index[None, :]).astype(jnp.bfloat16)
+    marks = jnp.broadcast_to((dest_local + 1)[:, None], (row_total, LANES)).astype(jnp.bfloat16)
     send_rows = jnp.dot(
-        slot_pick.astype(jnp.bfloat16), image_rows, preferred_element_type=jnp.float32
+        slot_pick,
+        jnp.concatenate([image_rows, marks], axis=1),
+        preferred_element_type=jnp.float32,
     ).astype(jnp.bfloat16)
-    send_pos = jnp.sum(jnp.where(slot_pick, dest_local[None, :] + 1, 0), axis=1) - 1
-    send_rows = send_rows.reshape(grp_count, SEND_CAP, image_rows.shape[1])
-    send_pos = send_pos.reshape(grp_count, SEND_CAP)
-    recv_rows, recv_pos = (
-        lax.all_to_all(send_rows, "grp", split_axis=0, concat_axis=0, tiled=True),
-        lax.all_to_all(send_pos, "grp", split_axis=0, concat_axis=0, tiled=True),
-    )
-    recv_rows = recv_rows.reshape(grp_count * SEND_CAP, image_rows.shape[1])
-    recv_pos = recv_pos.reshape(grp_count * SEND_CAP)
+    send_rows = send_rows.reshape(grp_count, SEND_CAP, width + LANES)
+    recv = lax.all_to_all(send_rows, "grp", split_axis=0, concat_axis=0, tiled=True)
+    recv = recv.reshape(grp_count * SEND_CAP, width + LANES)
+    recv_rows = recv[:, :width]
+    recv_pos = recv[:, width].astype(jnp.int32) - 1
     position_hit = jnp.arange(tok_count, dtype=jnp.int32)[:, None] == recv_pos[None, :]
     placed = jnp.dot(
         position_hit.astype(jnp.bfloat16), recv_rows, preferred_element_type=jnp.float32
     ).astype(jnp.bfloat16)
     covered = jnp.any(position_hit, axis=1)
     prompt = jnp.where(covered[:, None], placed, text)
-    token_normed = layer_norm(prompt)
-    all_tokens, all_segments = (
-        lax.all_gather(token_normed, "tp", axis=0, tiled=True),
-        lax.all_gather(segments, "tp", axis=1, tiled=True),
-    )
-    heads_txt = attention_heads(all_tokens, txt_qkv, all_segments[0], True)
-    own_text = lax.all_to_all(heads_txt, "tp", split_axis=0, concat_axis=1, tiled=True)
-    return (prompt.astype(jnp.float32) + project_out(own_text, txt_out)).astype(jnp.bfloat16)
+    return attention_layer(prompt, segments, txt_qkv, txt_out, True, 4)
 
 
 def solution(mesh):

time: 398 us -> 228 us (0.57)
  waiting for transfers between devices: 242 us -> 13.2 us
  Pallas kernels: 0 us -> 142 us
  blocking collectives: 32.9 us -> 0 us
  starting transfers between devices: 31.8 us -> 7.05 us
  between operations: 13.5 us -> 0.56 us
  local copies, waits for them, and re-layouts: 18.5 us -> 9.51 us
    all_gather x5 -> x0, waiting for transfers between devices: 217 us -> none  [the longest x2 125 us: project_out(): lax.all_gather(columns, 'grp', axis=1, tiled=True)]
    pallas_call x0 -> x6, Pallas kernels: none -> 142 us  [the longest x3 110 us: gather_rows(): pl.pallas_call(functools.partial(gather_kernel, with_extras), out_shape=s...]
    all_gather x2 -> x0, blocking collectives: 32.9 us -> none  [the longest x1 17.3 us: per_device(): lax.all_gather(pictures, 'tp', axis=1, tiled=True)]
    all_to_all x4 -> x0, starting transfers between devices: 26.8 us -> none  [the longest x1 10.8 us: per_device(): lax.all_to_all(send_pos, 'grp', split_axis=0, concat_axis=0, tiled=True)]
    all_to_all x4 -> x0, waiting for transfers between devices: 13 us -> none  [the longest x1 8.03 us: per_device(): lax.all_to_all(send_pos, 'grp', split_axis=0, concat_axis=0, tiled=True)]
    unnamed x28 -> x38, local copies, waits for them, and re-layouts: 12.6 us -> 0.98 us
  transfers between devices with their start and end apart: 10 -> 1, of which waited for: 8 -> 1; matrix products, arithmetic and copies ran while one was open for 14% -> 0% of each run, Pallas kernels for 0% -> 0%
where the time goes in v1:
time: 228 us; the launch traced here: 226 us
  Pallas kernels  142 us (62%)
  matrix products  43.1 us (19%)
  waiting for transfers between devices  13.2 us (6%)
  other arithmetic  10.4 us (5%)
  local copies, waits for them, and re-layouts  9.51 us (4%)
  starting transfers between devices  7.05 us (3%)
    pallas_call x3, Pallas kernels, gather_rows(): pl.pallas_call(functools.partial(gather_kernel, with_extras), out_shape=s...  110 us
    pallas_call x3, Pallas kernels, swap_blocks(): pl.pallas_call(functools.partial(swap_kernel, with_shards), out_shape=[ja...  32 us
    sub x4, matrix products, local_attention(): weights = jnp.exp(scores - row_max)  14.9 us
    dot_general x7, matrix products, times_transpose(): lax.dot_general(left, right, (((1,), (1,)), ((), ())), preferred_element_...  13.3 us
    all_to_all x1, waiting for transfers between devices, per_device(): lax.all_to_all(send_rows, 'grp', split_axis=0, concat_axis=0, tiled=True)  13.2 us
    dot_general x4, matrix products, local_attention(): jnp.einsum('hqk,khd->qhd', prob_bf, v_heads[:end_key], preferred_element_...  8.28 us
    all_to_all x1, starting transfers between devices, per_device(): lax.all_to_all(send_rows, 'grp', split_axis=0, concat_axis=0, tiled=True)  7.05 us
    dot_general x4, matrix products, project(): return jnp.dot(flat, own_heads, preferred_element_type=jnp.float32)  6.12 us
  transfers between devices with their start and end apart: 1, of which 1 were waited for; matrix products, arithmetic and copies ran while one was open for 0% of the time, Pallas kernels for 0%

profile of v1, /device:TPU:56, one launch (start us, length us, event | category | flops | bytes accessed | tf_op | source)
XLA Modules:
  0.0 225.6 jit_solution(8664377865817876093)
XLA Ops:
  0.0 1.2 convert_reduce_fusion
  1.2 1.2 fusion.34
  2.4 1.9 fusion.35.refs_0_
  4.4 1.4 pad.7.refs_2_
  5.8 41.8 %shard_map.100 = (bf16[8,128,1280]{2,1,0:T(8,128)(2,1)}, s32[8,1,128]{2,1,0:T(1,128)}, bf16[8,4,24,1280]{3,2,1,0:T(8,128)(2,1)}) custom-call(bf16[128,1280]{1,0:T(8,128)(2,1)} %fusion.35.refs_0_, s32[1,128]{1,0:T(1,128)} %refs_1_.2, bf16[24,1280]{1,0:T(8,128)(2,1)} %pad.7.refs_2_), custom_call_target="tpu_custom_call" | custom-call | tf_op jit(solution)/shard_map/pallas_call | solution.py:186
  47.6 3.7 %convolution_convert_fusion.5 = bf16[1024,160]{0,1:T(8,128)(2,1)} fusion(bf16[1024,1280]{1,0:T(8,128)(2,1)} %bitcast.158, bf16[3,160,1280]{2,1,0:T(8,128)(2,1)} %param.12), kind=kOutput, calls=%fused_computation.41 | convolution fusion | flops 419594240 | bytes 3358720 | tf_op jit(solution)/shard_map/dot_general | solution.py:34
  51.3 1.0 convolution_convert_fusion.6
  52.3 1.0 convolution_convert_fusion.7
  53.6 0.7 broadcast_compare_fusion.1
  54.2 4.6 %fusion.89 = (f32[2,512]{1,0:T(2,128)S(1)}, f32[2,512,1024]{2,1,0:T(8,128)}) fusion(pred[512,1024]{1,0:T(8,128)(4,1)S(1)} %get-tuple-element.37, bf16[512,2,80]{0,2,1:T(8,128)(2,1)S(1)} %bitcast.139, bf16[1024,2,80]{0,2,1:T(8,128)(2,1)} %bitcast.166), kind=kOutput, calls=%fused_computation.147 | convolution fusion | flops 171967488 | bytes 5214208 | tf_op jit(solution)/shard_map/sub | solution.py:294
  58.9 4.6 %fusion.88 = (f32[2,512]{1,0:T(2,128)S(1)}, f32[2,512,1024]{2,1,0:T(8,128)}) fusion(pred[512,1024]{1,0:T(8,128)(4,1)S(1)} %get-tuple-element.38, bf16[512,2,80]{0,2,1:T(8,128)(2,1)S(1)} %bitcast.137, bf16[1024,2,80]{0,2,1:T(8,128)(2,1)} %bitcast.167), kind=kOutput, calls=%fused_computation.146 | convolution fusion | flops 171967488 | bytes 5214208 | tf_op jit(solution)/shard_map/sub | solution.py:294
  63.5 3.2 %fusion.25 = bf16[2,80,512]{2,1,0:T(8,128)(2,1)S(1)} fusion(bf16[1024,2,80]{0,2,1:T(8,128)(2,1)S(1)} %bitcast.164, f32[2,512,1024]{2,1,0:T(8,128)} %get-tuple-element.46, f32[2,512]{1,0:T(2,128)S(1)} %get-tuple-element.45), kind=kOutput, calls=%fused_computation.47 | convolution fusion | flops 169951232 | bytes 4689920 | tf_op jit(solution)/shard_map/hqk,khd->qhd/dot_general | solution.py:296
  66.7 0.3 copy-done.18
  66.9 0.8 fusion.24
  67.8 0.8 bitcast_bitcast_fusion.1.refs_0_
  68.6 11.7 %shard_map.101 = (bf16[8,160,128]{2,1,0:T(8,128)(2,1)}, bf16[8,4,24,1280]{3,2,1,0:T(8,128)(2,1)}) custom-call(bf16[8,160,128]{2,1,0:T(8,128)(2,1)} %bitcast_bitcast_fusion.1.refs_0_, bf16[8,4,24,1280]{3,2,1,0:T(8,128)(2,1)} %get-tuple-element.15.refs_1_), custom_call_target="tpu_custom_call" | custom-call | tf_op jit(solution)/shard_map/pallas_call | solution.py:255
  80.3 2.4 %fusion.93 = f32[768,128]{1,0:T(8,128)S(1)} fusion(bf16[768,1280]{1,0:T(8,128)(2,1)} %bitcast.124, bf16[1280,128]{1,0:T(8,128)(2,1)} %bitcast.132), kind=kOutput, calls=%fused_computation.151 | convolution fusion | flops 251658240 | bytes 2686976 | tf_op jit(solution)/shard_map/dot_general | solution.py:323
  82.7 0.7 broadcast_select_fusion.3
  83.8 0.6 copy-done.3
  84.5 0.2 fusion.36
  85.0 0.9 reshape.343.refs_0_
  85.9 32.0 %shard_map.102 = bf16[8,32,5120]{2,1,0:T(8,128)(2,1)} custom-call(bf16[32,5120]{1,0:T(8,128)(2,1)} %reshape.343.refs_0_), custom_call_target="tpu_custom_call" | custom-call | tf_op jit(solution)/shard_map/pallas_call | solution.py:186
  118.0 2.8 %convolution_convert_fusion.9 = bf16[256,160]{0,1:T(8,128)(2,1)S(1)} fusion(bf16[256,5120]{1,0:T(8,128)(2,1)} %bitcast.121, bf16[160,5120]{1,0:T(8,128)(2,1)S(1)} %copy-done), kind=kOutput, calls=%fused_computation.48 | convolution fusion | flops 419471360 | bytes 4341760 | tf_op jit(solution)/shard_map/dot_general | solution.py:34
  120.8 0.8 copy.44
  121.5 9.6 %shard_map.103 = bf16[8,32,160]{2,1,0:T(8,128)(2,1)} custom-call(bf16[8,32,160]{2,1,0:T(8,128)(2,1)} %bitcast.134), custom_call_target="tpu_custom_call" | custom-call | tf_op jit(solution)/shard_map/pallas_call | solution.py:255
  131.1 1.0 copy.45
  132.6 0.9 reshape.347
  133.5 7.0 %all-to-all-start = ((bf16[64,2,1408]{2,1,0:T(2,128)(2,1)}), bf16[64,2,1408]{2,1,0:T(2,128)(2,1)S(1)}, u32[]{:S(2)}, u32[]{:S(2)}) async-start(bf16[64,2,1408]{2,1,0:T(2,128)(2,1)} %reshape.347), calls=%async_computation | async-start | bytes 720896 | tf_op jit(solution)/shard_map/all_to_all | solution.py:366
  140.5 0.6 pad.8.refs_2_
  141.2 13.2 %all-to-all-done = bf16[64,2,1408]{2,1,0:T(2,128)(2,1)S(1)} async-done(((bf16[64,2,1408]{2,1,0:T(2,128)(2,1)}), bf16[64,2,1408]{2,1,0:T(2,128)(2,1)S(1)}, u32[]{:S(2)}, u32[]{:S(2)}) %all-to-all-start) | async-done | bytes 360480 | tf_op jit(solution)/shard_map/all_to_all | solution.py:366
  154.7 0.3 fusion.90
  155.3 0.9 multiply_convert_fusion.refs_0_
  156.2 35.9 %shard_map.104 = (bf16[8,128,1280]{2,1,0:T(8,128)(2,1)}, s32[8,1,128]{2,1,0:T(1,128)}, bf16[8,4,24,1280]{3,2,1,0:T(8,128)(2,1)}) custom-call(bf16[128,1280]{1,0:T(8,128)(2,1)} %multiply_convert_fusion.refs_0_, s32[1,128]{1,0:T(1,128)} %refs_1_.3, bf16[24,1280]{1,0:T(8,128)(2,1)} %pad.8.refs_2_), custom_call_target="tpu_custom_call" | custom-call | tf_op jit(solution)/shard_map/pallas_call | solution.py:186
  192.1 2.9 %convolution_convert_fusion.2 = bf16[1024,160]{0,1:T(8,128)(2,1)S(1)} fusion(bf16[1024,1280]{1,0:T(8,128)(2,1)} %bitcast.161, bf16[3,160,1280]{2,1,0:T(8,128)(2,1)} %param.18), kind=kOutput, calls=%fused_computation.38 | convolution fusion | flops 419594240 | bytes 3358720 | tf_op jit(solution)/shard_map/dot_general | solution.py:34
  195.1 1.0 convolution_convert_fusion.4
  196.1 1.0 convolution_convert_fusion.3
  197.4 1.0 fusion.92
  198.4 1.2 convolution_convert_fusion.8
  199.7 0.6 fusion.15
  200.3 4.6 %fusion.91 = (f32[2,512]{1,0:T(2,128)S(1)}, f32[2,512,1024]{2,1,0:T(8,128)}) fusion(pred[512,1024]{1,0:T(8,128)(4,1)S(1)} %fusion.15, bf16[512,2,80]{0,2,1:T(8,128)(2,1)S(1)} %bitcast.138, bf16[1024,2,80]{0,2,1:T(8,128)(2,1)} %bitcast.149), kind=kOutput, calls=%fused_computation.149 | convolution fusion | flops 171967488 | bytes 5214208 | tf_op jit(solution)/shard_map/sub | solution.py:294
  204.9 3.0 %fusion.23 = bf16[2,80,512]{2,1,0:T(8,128)(2,1)S(1)} fusion(bf16[1024,2,80]{0,2,1:T(8,128)(2,1)S(1)} %bitcast.147, f32[2,512,1024]{2,1,0:T(8,128)} %get-tuple-element.50, f32[2,512]{1,0:T(2,128)S(1)} %get-tuple-element.49), kind=kOutput, calls=%fused_computation.45 | convolution fusion | flops 169951232 | bytes 4689920 | tf_op jit(solution)/shard_map/hqk,khd->qhd/dot_general | solution.py:296
  208.0 0.8 bitcast_bitcast_fusion.refs_0_
  208.7 10.7 %shard_map.105 = (bf16[8,160,128]{2,1,0:T(8,128)(2,1)}, bf16[8,4,24,1280]{3,2,1,0:T(8,128)(2,1)}) custom-call(bf16[8,160,128]{2,1,0:T(8,128)(2,1)} %bitcast_bitcast_fusion.refs_0_, bf16[8,4,24,1280]{3,2,1,0:T(8,128)(2,1)} %get-tuple-element.20.refs_1_), custom_call_target="tpu_custom_call" | custom-call | tf_op jit(solution)/shard_map/pallas_call | solution.py:255
  219.4 2.4 %fusion.94 = f32[768,128]{1,0:T(8,128)S(1)} fusion(bf16[768,1280]{1,0:T(8,128)(2,1)} %bitcast.125, bf16[1280,128]{1,0:T(8,128)(2,1)} %bitcast.130), kind=kOutput, calls=%fused_computation.152 | convolution fusion | flops 251658240 | bytes 2686976 | tf_op jit(solution)/shard_map/dot_general | solution.py:323
  221.8 0.7 broadcast_select_fusion.1
  222.6 0.9 reshape.358
  223.5 1.3 copy.50
  224.8 0.8 add_convert_fusion
  (67 shorter events, 2.4 us)
Async XLA Ops:
  0.0 118.0 %copy-start = (bf16[160,5120]{1,0:T(8,128)(2,1)S(1)}, bf16[160,5120]{1,0:T(8,128)(2,1)}, u32[]{:S(2)}) copy-start(bf16[160,5120]{1,0:T(8,128)(2,1)} %param.14) | copy-start | bytes 4915204
  47.6 3.7 %copy-start.13 = (bf16[8,128,1280]{2,1,0:T(8,128)(2,1)S(1)}, bf16[8,128,1280]{2,1,0:T(8,128)(2,1)}, u32[]{:S(2)}) copy-start(bf16[8,128,1280]{2,1,0:T(8,128)(2,1)} %get-tuple-element.16) | copy-start | bytes 7864324
  47.6 3.7 %copy-start.15 = (bf16[3,160,1280]{2,1,0:T(8,128)(2,1)S(1)}, bf16[3,160,1280]{2,1,0:T(8,128)(2,1)}, u32[]{:S(2)}) copy-start(bf16[3,160,1280]{2,1,0:T(8,128)(2,1)} %param.12) | copy-start | bytes 3686404
  52.3 1.0 copy-start.17
  52.3 1.2 copy-start.11
  63.5 3.4 %copy-start.18 = (f32[2,512,1024]{2,1,0:T(8,128)S(1)}, f32[2,512,1024]{2,1,0:T(8,128)}, u32[]{:S(2)}) copy-start(f32[2,512,1024]{2,1,0:T(8,128)} %get-tuple-element.44) | copy-start | bytes 12582916
  80.3 2.4 %copy-start.1 = (bf16[8,4,24,1280]{3,2,1,0:T(8,128)(2,1)S(1)}, bf16[8,4,24,1280]{3,2,1,0:T(8,128)(2,1)}, u32[]{:S(2)}) copy-start(bf16[8,4,24,1280]{3,2,1,0:T(8,128)(2,1)} %get-tuple-element.15.refs_1_) | copy-start | bytes 5898244
  80.3 2.4 %copy-start.5 = (bf16[8,160,128]{2,1,0:T(8,128)(2,1)S(1)}, bf16[8,160,128]{2,1,0:T(8,128)(2,1)}, u32[]{:S(2)}) copy-start(bf16[8,160,128]{2,1,0:T(8,128)(2,1)} %get-tuple-element.18) | copy-start | bytes 983044
  83.4 1.0 copy-start.3
  120.7 19.8 %copy-start.10 = (bf16[1280,20]{0,1:T(8,128)(2,1)S(1)}, bf16[1280,20]{0,1:T(8,128)(2,1)}, u32[]{:S(2)}) copy-start(bf16[1280,20]{0,1:T(8,128)(2,1)} %param.19) | copy-start | bytes 153604
  120.7 34.0 %copy-start.6 = (bf16[128,1280]{1,0:T(8,128)(2,1)S(1)}, bf16[128,1280]{1,0:T(8,128)(2,1)}, u32[]{:S(2)}) copy-start(bf16[128,1280]{1,0:T(8,128)(2,1)} %param.15) | copy-start | bytes 983044
  133.5 20.9 %all-to-all-start = ((bf16[64,2,1408]{2,1,0:T(2,128)(2,1)}), bf16[64,2,1408]{2,1,0:T(2,128)(2,1)S(1)}, u32[]{:S(2)}, u32[]{:S(2)}) async-start(bf16[64,2,1408]{2,1,0:T(2,128)(2,1)} %reshape.347), calls=%async_computation | async-start | bytes 720896 | tf_op jit(solution)/shard_map/all_to_all | solution.py:366
  192.1 3.0 %copy-start.14 = (bf16[8,128,1280]{2,1,0:T(8,128)(2,1)S(1)}, bf16[8,128,1280]{2,1,0:T(8,128)(2,1)}, u32[]{:S(2)}) copy-start(bf16[8,128,1280]{2,1,0:T(8,128)(2,1)} %get-tuple-element.21) | copy-start | bytes 7864324
  192.1 3.0 %copy-start.16 = (bf16[3,160,1280]{2,1,0:T(8,128)(2,1)S(1)}, bf16[3,160,1280]{2,1,0:T(8,128)(2,1)}, u32[]{:S(2)}) copy-start(bf16[3,160,1280]{2,1,0:T(8,128)(2,1)} %param.18) | copy-start | bytes 3686404
  195.1 2.2 copy-start.9
  196.1 1.3 copy-start.7
  196.1 1.0 copy-start.12
  197.4 1.0 slice-start
  200.3 4.7 %copy-start.8 = (bf16[1024,160]{0,1:T(8,128)(2,1)S(1)}, bf16[1024,160]{0,1:T(8,128)(2,1)}, u32[]{:S(2)}) copy-start(bf16[1024,160]{0,1:T(8,128)(2,1)} %copy-done.7) | copy-start | bytes 983044
  219.4 2.4 %copy-start.2 = (bf16[8,4,24,1280]{3,2,1,0:T(8,128)(2,1)S(1)}, bf16[8,4,24,1280]{3,2,1,0:T(8,128)(2,1)}, u32[]{:S(2)}) copy-start(bf16[8,4,24,1280]{3,2,1,0:T(8,128)(2,1)} %get-tuple-element.20.refs_1_) | copy-start | bytes 5898244
  219.4 2.4 %copy-start.4 = (bf16[8,160,128]{2,1,0:T(8,128)(2,1)S(1)}, bf16[8,160,128]{2,1,0:T(8,128)(2,1)}, u32[]{:S(2)}) copy-start(bf16[8,160,128]{2,1,0:T(8,128)(2,1)} %get-tuple-element.23) | copy-start | bytes 983044

commit v2 on v1

--- a/solution.py
+++ b/solution.py
@@ -262,59 +262,197 @@
     )(*operands)
 
 
-def local_attention(queries, key_rows, value_rows, labels, causal):
-    row_count, col_count = queries.shape
-    heads_here = col_count // HEAD_DIM
-    q_heads = queries.reshape(row_count, heads_here, HEAD_DIM)
-    k_heads = key_rows.reshape(row_count, heads_here, HEAD_DIM)
-    v_heads = value_rows.reshape(row_count, heads_here, HEAD_DIM)
-    blocks = max(1, min(8, row_count // 512))
-    block_rows = row_count // blocks
-    inv_root = HEAD_DIM ** (-0.5)
-    outputs = []
-    for block_index in range(blocks):
-        begin_row = block_index * block_rows
-        end_key = begin_row + block_rows if causal else row_count
-        scores = (
-            jnp.einsum(
-                "qhd,khd->hqk",
-                q_heads[begin_row : begin_row + block_rows],
-                k_heads[:end_key],
+Q_BLOCK = 256
+
+
+def project_all(rows, weights):
+    return lax.dot_general(
+        weights, rows, (((1,), (1,)), ((), ())), preferred_element_type=jnp.float32
+    )
+
+
+def attend(projected, labels, store, causal):
+    heads_here = projected.shape[0] // 3 // HEAD_DIM
+    row_count = projected.shape[1]
+    factor = HEAD_DIM ** (-0.5) * 1.4426950408889634
+    key_labels = jnp.concatenate(
+        [jnp.broadcast_to(label, (LANES, LANES)).T for label in labels], axis=0
+    )
+    keys = []
+    for head in range(heads_here):
+        begin = (heads_here + head) * HEAD_DIM
+        keys.append(projected[begin : begin + HEAD_DIM].T.astype(jnp.bfloat16))
+    lanes_per = Q_BLOCK // LANES
+    for block in range(row_count // Q_BLOCK):
+        first = block * Q_BLOCK
+        end_key = first + Q_BLOCK if causal else row_count
+        allowed = jnp.concatenate(
+            [
+                key_labels[:end_key] == labels[block * lanes_per + piece]
+                for piece in range(lanes_per)
+            ],
+            axis=1,
+        )
+        if causal:
+            key_ids = lax.broadcasted_iota(jnp.int32, (end_key, Q_BLOCK), 0)
+            query_ids = lax.broadcasted_iota(jnp.int32, (end_key, Q_BLOCK), 1) + first
+            allowed = allowed & (query_ids >= key_ids)
+        for head in range(heads_here):
+            begin = head * HEAD_DIM
+            queries = projected[begin : begin + HEAD_DIM, first : first + Q_BLOCK]
+            value_begin = (2 * heads_here + head) * HEAD_DIM
+            values = projected[value_begin : value_begin + HEAD_DIM, :end_key]
+            scores = jnp.dot(
+                keys[head][:end_key],
+                queries.astype(jnp.bfloat16),
                 preferred_element_type=jnp.float32,
             )
-            * inv_root
+            scores = jnp.where(allowed, scores, MASKED)
+            top = jnp.max(scores, axis=0, keepdims=True)
+            weights = jnp.exp2((scores - top) * factor)
+            total = jnp.sum(weights, axis=0, keepdims=True)
+            mixed = jnp.dot(
+                values.astype(jnp.bfloat16),
+                weights.astype(jnp.bfloat16),
+                preferred_element_type=jnp.float32,
+            )
+            store(block, head, (mixed / total).astype(jnp.bfloat16))
+
+
+def attention_kernel(causal, rows, weights, labels, out, projected):
+    projected[...] = project_all(rows[...], weights[...])
+    label_rows = [labels[part].astype(jnp.float32) for part in range(N_TP)]
+
+    def store(block, head, mixed):
+        for piece in range(Q_BLOCK // LANES):
+            target = block * (Q_BLOCK // LANES) + piece
+            out[target, head * HEAD_DIM : (head + 1) * HEAD_DIM, :] = mixed[
+                :, piece * LANES : (piece + 1) * LANES
+            ]
+
+    attend(projected, label_rows, store, causal)
+
+
+def attention_heads(gathered, weights, labels, causal):
+    features = weights.shape[0] * weights.shape[1]
+    vmem = pl.BlockSpec(memory_space=pltpu.VMEM)
+    return pl.pallas_call(
+        functools.partial(attention_kernel, causal),
+        out_shape=jax.ShapeDtypeStruct((N_TP, weights.shape[1], LANES), jnp.bfloat16),
+        in_specs=[vmem] * 3,
+        out_specs=vmem,
+        scratch_shapes=[pltpu.VMEM((features, gathered.shape[0]), jnp.float32)],
+    )(gathered, weights.reshape(features, weights.shape[2]), labels)
+
+
+def merge_kernel(own, weights_hbm, image, slots, weights, results, *sems):
+    row_send, row_recv, col_send, col_recv, local_sem = sems
+    tp = lax.axis_index("tp")
+    half = own.shape[0] // 2
+    greet([{"tp": wrap(tp + d, N_TP)} for d in range(1, N_TP)])
+    neighbours = [{"tp": wrap(tp + 1, N_TP)}, {"tp": wrap(tp - 1, N_TP)}]
+
+    def block_of(way, step):
+        return wrap(tp - step, N_TP) if way == 0 else wrap(tp + step, N_TP)
+
+    def row_copy(way, step, part):
+        span = pl.ds(part * half, half)
+        dst = slots.at[block_of(way, step), span]
+        slot = (way * 4 + step) * 2 + part
+        return pltpu.make_async_remote_copy(
+            src_ref=own.at[span] if step == 0 else dst,
+            dst_ref=dst,
+            send_sem=row_send.at[slot],
+            recv_sem=row_recv.at[slot],
+            device_id=neighbours[way],
+            device_id_type=MESH,
         )
-        allowed = labels[begin_row : begin_row + block_rows, None] == labels[None, :end_key]
-        if causal:
-            query_ids = jnp.arange(begin_row, begin_row + block_rows, dtype=jnp.int32)
-            key_ids = jnp.arange(end_key, dtype=jnp.int32)
-            allowed = allowed & (query_ids[:, None] >= key_ids[None, :])
-        scores = jnp.where(allowed[None], scores, MASKED)
-        row_max = jnp.max(scores, axis=-1, keepdims=True)
-        weights = jnp.exp(scores - row_max)
-        prob_bf = (weights / jnp.sum(weights, axis=-1, keepdims=True)).astype(jnp.bfloat16)
-        mixed = jnp.einsum(
-            "hqk,khd->qhd", prob_bf, v_heads[:end_key], preferred_element_type=jnp.float32
+
+    pending = []
+    ring = {}
+
+    def start(way, step, part):
+        ring[way, step, part] = row_copy(way, step, part)
+        ring[way, step, part].start()
+        pending.append(ring[way, step, part])
+
+    for part in range(2):
+        for way in range(2):
+            start(way, 0, part)
+    fetch = pltpu.make_async_copy(weights_hbm, weights, local_sem.at[0])
+    fetch.start()
+    fetch.wait()
+
+    def columns(block):
+        return times_transpose(block, weights[...]).astype(jnp.bfloat16)
+
+    results[tp] = columns(own[...])
+    keep = pltpu.make_async_copy(results.at[tp], image.at[tp], local_sem.at[1])
+    keep.start()
+    arrivals = []
+
+    def give(way, step):
+        block = block_of(way, step)
+        results[block] = columns(slots[block])
+        copy = pltpu.make_async_remote_copy(
+            src_ref=results.at[block],
+            dst_ref=image.at[tp],
+            send_sem=col_send.at[way * 5 + step],
+            recv_sem=col_recv.at[way * 5 + step],
+            device_id={"tp": block},
+            device_id_type=MESH,
         )
-        outputs.append(mixed.astype(jnp.bfloat16).reshape(block_rows, col_count))
-    return jnp.concatenate(outputs, axis=0)
-
-
-def attention_heads(gathered, weights, labels, causal):
-    queries = times_transpose(gathered, weights[0]).astype(jnp.bfloat16)
-    key_rows = times_transpose(gathered, weights[1]).astype(jnp.bfloat16)
-    value_rows = times_transpose(gathered, weights[2]).astype(jnp.bfloat16)
-    return local_attention(queries, key_rows, value_rows, labels, causal)
+        copy.start()
+        pending.append(copy)
+        arrivals.append(copy)
+
+    for step in range(1, 4):
+        for part in range(2):
+            for way in range(2):
+                ring[way, step - 1, part].wait_recv()
+                if step < 3 or part == way:
+                    start(way, step, part)
+        for way in range(2):
+            give(way, step)
+    for way in range(2):
+        ring[way, 3, way].wait_recv()
+    give(0, 4)
+    keep.wait()
+    for copy in arrivals:
+        copy.wait_recv()
+    for copy in pending:
+        copy.wait_send()
+
+
+def merge_rows(merged, merge_w, collective_id):
+    row_total, depth = merged.shape
+    features = merge_w.shape[0]
+    hbm = pl.BlockSpec(memory_space=pl.ANY)
+    dma = pltpu.SemaphoreType.DMA
+    return pl.pallas_call(
+        merge_kernel,
+        out_shape=jax.ShapeDtypeStruct((N_TP, row_total, features), jnp.bfloat16),
+        in_specs=[pl.BlockSpec(memory_space=pltpu.VMEM), hbm],
+        out_specs=hbm,
+        scratch_shapes=[
+            pltpu.VMEM((N_TP, row_total, depth), jnp.bfloat16),
+            pltpu.VMEM((features, depth), jnp.bfloat16),
+            pltpu.VMEM((N_TP, row_total, features), jnp.bfloat16),
+            dma((16,)),
+            dma((16,)),
+            dma((10,)),
+            dma((10,)),
+            dma((2,)),
+        ],
+        compiler_params=pltpu.CompilerParams(collective_id=collective_id, has_side_effects=True),
+    )(merged, merge_w)
 
 
 def attention_layer(rows, labels, qkv, columns, causal, first_id):
     shard = jnp.pad(columns.T, ((0, SHARD_PAD - SHARD), (0, 0)))
     gathered, all_labels, shards = gather_rows(layer_norm(rows), first_id, labels, shard)
     row_total = N_TP * rows.shape[0]
-    heads = attention_heads(
-        gathered.reshape(row_total, rows.shape[1]), qkv, all_labels.reshape(row_total), causal
-    )
-    blocks = heads.reshape(N_TP, rows.shape[0], heads.shape[1]).transpose(0, 2, 1)
+    blocks = attention_heads(gathered.reshape(row_total, rows.shape[1]), qkv, all_labels, causal)
     own_heads, other = swap_blocks(blocks, first_id + 1, shards)
     own_heads = own_heads.reshape(rows.shape[1], rows.shape[0])
 
@@ -338,12 +476,8 @@
     width = patches.shape[1]
     vis_hidden = attention_layer(patches, pictures, vis_qkv, vis_out, False, 0)
     merged = layer_norm(vis_hidden).reshape(patches.shape[0] // 4, 4 * width)
-    (all_merged,) = gather_rows(merged, 2)
     row_total = places.shape[0]
-    image_cols = times_transpose(
-        all_merged.reshape(tp_count * row_total, 4 * width), merge_w
-    ).astype(jnp.bfloat16)
-    (image_parts,) = swap_blocks(image_cols.reshape(tp_count, row_total, -1), 3)
+    image_parts = merge_rows(merged, merge_w, 2)
     image_rows = image_parts.transpose(1, 0, 2).reshape(row_total, width)
     tok_count = text.shape[0]
     group_tokens = tok_count * tp_count

time: 228 us -> 203 us (0.89)
  matrix products: 43.1 us -> 6.65 us
  Pallas kernels: 142 us -> 161 us
  local copies, waits for them, and re-layouts: 9.51 us -> 6.48 us
  other arithmetic: 10.4 us -> 7.95 us
    pallas_call x0 -> x3, Pallas kernels: none -> 58.8 us  [the longest x1 41 us: merge_rows(): pl.pallas_call(merge_kernel, out_shape=jax.ShapeDtypeStruct((N_TP, row_to...]
    pallas_call x3 -> x2, Pallas kernels: 110 us -> 77.7 us  [gather_rows(): pl.pallas_call(functools.partial(gather_kernel, with_extras), out_shape=s...]
    dot_general x11 -> x0, matrix products: 21.6 us -> none  [the longest x7 13.3 us: times_transpose(): lax.dot_general(left, right, (((1,), (1,)), ((), ())), preferred_element_...]
    sub x4 -> x0, matrix products: 14.9 us -> none  [local_attention(): weights = jnp.exp(scores - row_max)]
    pallas_call x3 -> x2, Pallas kernels: 32 us -> 24.1 us  [swap_blocks(): pl.pallas_call(functools.partial(swap_kernel, with_shards), out_shape=[ja...]
where the time goes in v2:
time: 203 us; the launch traced here: 201 us
  Pallas kernels  161 us (79%)
  waiting for transfers between devices  13.2 us (7%)
  other arithmetic  7.95 us (4%)
  matrix products  6.65 us (3%)
  local copies, waits for them, and re-layouts  6.48 us (3%)
  starting transfers between devices  5.83 us (3%)
    pallas_call x2, Pallas kernels, gather_rows(): pl.pallas_call(functools.partial(gather_kernel, with_extras), out_shape=s...  77.7 us
    pallas_call x1, Pallas kernels, merge_rows(): pl.pallas_call(merge_kernel, out_shape=jax.ShapeDtypeStruct((N_TP, row_to...  41 us
    pallas_call x2, Pallas kernels, swap_blocks(): pl.pallas_call(functools.partial(swap_kernel, with_shards), out_shape=[ja...  24.1 us
    pallas_call x2, Pallas kernels, attention_heads(): pl.pallas_call(functools.partial(attention_kernel, causal), out_shape=jax...  17.7 us
    all_to_all x1, waiting for transfers between devices, per_device(): lax.all_to_all(send_rows, 'grp', split_axis=0, concat_axis=0, tiled=True)  13.2 us
    dot_general x4, matrix products, project(): return jnp.dot(flat, own_heads, preferred_element_type=jnp.float32)  5.91 us
    all_to_all x1, starting transfers between devices, per_device(): lax.all_to_all(send_rows, 'grp', split_axis=0, concat_axis=0, tiled=True)  5.83 us
  transfers between devices with their start and end apart: 1, of which 1 were waited for; matrix products, arithmetic and copies ran while one was open for 0% of the time, Pallas kernels for 0%

profile of v2, /device:TPU:56, one launch (start us, length us, event | category | flops | bytes accessed | tf_op | source)
XLA Modules:
  0.0 200.9 jit_solution(9518148878476988735)
XLA Ops:
  0.0 1.1 convert_reduce_fusion
  1.1 1.2 fusion.6
  2.3 0.7 and_select_fusion.1
  3.0 0.2 convert_reduce_fusion.2
  3.2 1.9 fusion.7.refs_0_
  5.1 1.5 pad.7.refs_2_
  6.6 41.8 %shard_map.100 = (bf16[8,128,1280]{2,1,0:T(8,128)(2,1)}, s32[8,1,128]{2,1,0:T(1,128)}, bf16[8,4,24,1280]{3,2,1,0:T(8,128)(2,1)}) custom-call(bf16[128,1280]{1,0:T(8,128)(2,1)} %fusion.7.refs_0_, s32[1,128]{1,0:T(1,128)} %refs_1_.2, bf16[24,1280]{1,0:T(8,128)(2,1)} %pad.7.refs_2_), custom_call_target="tpu_custom_call" | custom-call | tf_op jit(solution)/shard_map/pallas_call | solution.py:186
  48.3 9.8 %shard_map.101.refs_0_ = bf16[8,160,128]{2,1,0:T(8,128)(2,1)} custom-call(bf16[1024,1280]{1,0:T(8,128)(2,1)} %bitcast.35, bf16[480,1280]{1,0:T(8,128)(2,1)} %bitcast.47, s32[8,1,128]{2,1,0:T(1,128)} %get-tuple-element.17.labels), custom_call_target="tpu_custom_call" | custom-call | tf_op jit(solution)/shard_map/pallas_call | solution.py:339
  58.1 11.8 %shard_map.102 = (bf16[8,160,128]{2,1,0:T(8,128)(2,1)}, bf16[8,4,24,1280]{3,2,1,0:T(8,128)(2,1)}) custom-call(bf16[8,160,128]{2,1,0:T(8,128)(2,1)} %shard_map.101.refs_0_, bf16[8,4,24,1280]{3,2,1,0:T(8,128)(2,1)} %get-tuple-element.15.refs_1_), custom_call_target="tpu_custom_call" | custom-call | tf_op jit(solution)/shard_map/pallas_call | solution.py:255
  70.0 0.0 copy-start.4
  70.0 2.3 %fusion.24 = f32[768,128]{1,0:T(8,128)S(1)} fusion(bf16[768,1280]{1,0:T(8,128)(2,1)} %bitcast.37, bf16[1280,128]{1,0:T(8,128)(2,1)} %bitcast.45), kind=kOutput, calls=%fused_computation.59 | convolution fusion | flops 251658240 | bytes 2686976 | tf_op jit(solution)/shard_map/dot_general | solution.py:461
  72.3 0.0 copy-done.1
  72.3 0.0 copy-done.4
  72.3 0.7 broadcast_select_fusion.3
  73.0 0.0 copy-start.2
  73.0 0.1 copy_bitcast_fusion.1
  73.0 0.1 reshape.113
  73.1 0.2 copy.32
  73.3 0.6 copy-done.2
  73.9 0.2 convert_reduce_fusion.1
  74.1 0.2 fusion.8
  74.4 0.2 fusion.9
  74.6 0.9 reshape.114.own
  75.5 41.0 %shard_map.103 = bf16[8,32,160]{2,1,0:T(8,128)(2,1)} custom-call(bf16[32,5120]{1,0:T(8,128)(2,1)} %reshape.114.own, bf16[160,5120]{1,0:T(8,128)(2,1)} %weights_hbm.1), custom_call_target="tpu_custom_call" | custom-call | tf_op jit(solution)/shard_map/pallas_call | solution.py:432
  116.6 0.0 copy-start.5
  116.6 1.0 copy.33
  117.6 0.2 reshape.115
  117.8 0.1 broadcast_in_dim.7
  117.9 0.4 convolution_convert_fusion.1
  118.3 0.9 reshape.116
  119.1 5.8 %all-to-all-start = ((bf16[64,2,1408]{2,1,0:T(2,128)(2,1)}), bf16[64,2,1408]{2,1,0:T(2,128)(2,1)S(1)}, u32[]{:S(2)}, u32[]{:S(2)}) async-start(bf16[64,2,1408]{2,1,0:T(2,128)(2,1)} %reshape.116), calls=%async_computation | async-start | bytes 720896 | tf_op jit(solution)/shard_map/all_to_all | solution.py:500
  125.0 0.6 pad.8.refs_2_
  125.6 13.2 %all-to-all-done = bf16[64,2,1408]{2,1,0:T(2,128)(2,1)S(1)} async-done(((bf16[64,2,1408]{2,1,0:T(2,128)(2,1)}), bf16[64,2,1408]{2,1,0:T(2,128)(2,1)S(1)}, u32[]{:S(2)}, u32[]{:S(2)}) %all-to-all-start) | async-done | bytes 360480 | tf_op jit(solution)/shard_map/all_to_all | solution.py:500
  138.8 0.1 reshape.117
  138.9 0.1 add_reduce_fusion
  139.1 0.1 fusion.15
  139.2 0.3 fusion.23
  139.5 0.2 multiply_reduce_fusion
  139.7 0.9 multiply_convert_fusion.refs_0_
  140.6 35.9 %shard_map.104 = (bf16[8,128,1280]{2,1,0:T(8,128)(2,1)}, s32[8,1,128]{2,1,0:T(1,128)}, bf16[8,4,24,1280]{3,2,1,0:T(8,128)(2,1)}) custom-call(bf16[128,1280]{1,0:T(8,128)(2,1)} %multiply_convert_fusion.refs_0_, s32[1,128]{1,0:T(1,128)} %refs_1_.3, bf16[24,1280]{1,0:T(8,128)(2,1)} %pad.8.refs_2_), custom_call_target="tpu_custom_call" | custom-call | tf_op jit(solution)/shard_map/pallas_call | solution.py:186
  176.6 7.9 %shard_map.105.refs_0_ = bf16[8,160,128]{2,1,0:T(8,128)(2,1)} custom-call(bf16[1024,1280]{1,0:T(8,128)(2,1)} %bitcast.36, bf16[480,1280]{1,0:T(8,128)(2,1)} %bitcast.48, s32[8,1,128]{2,1,0:T(1,128)} %get-tuple-element.22.labels), custom_call_target="tpu_custom_call" | custom-call | tf_op jit(solution)/shard_map/pallas_call | solution.py:339
  184.5 12.3 %shard_map.106 = (bf16[8,160,128]{2,1,0:T(8,128)(2,1)}, bf16[8,4,24,1280]{3,2,1,0:T(8,128)(2,1)}) custom-call(bf16[8,160,128]{2,1,0:T(8,128)(2,1)} %shard_map.105.refs_0_, bf16[8,4,24,1280]{3,2,1,0:T(8,128)(2,1)} %get-tuple-element.20.refs_1_), custom_call_target="tpu_custom_call" | custom-call | tf_op jit(solution)/shard_map/pallas_call | solution.py:255
  196.8 2.3 %fusion.25 = f32[768,128]{1,0:T(8,128)S(1)} fusion(bf16[768,1280]{1,0:T(8,128)(2,1)} %bitcast.38, bf16[1280,128]{1,0:T(8,128)(2,1)} %bitcast.43), kind=kOutput, calls=%fused_computation.60 | convolution fusion | flops 251658240 | bytes 2686976 | tf_op jit(solution)/shard_map/dot_general | solution.py:461
  199.1 0.7 broadcast_select_fusion.1
  199.8 0.1 copy_bitcast_fusion
  199.8 0.1 reshape.123
  199.9 0.2 copy.36
  200.1 0.8 add_convert_fusion
  (15 shorter events, 0.1 us)
Async XLA Ops:
  58.1 14.1 %copy-start.1 = (bf16[8,4,24,1280]{3,2,1,0:T(8,128)(2,1)S(1)}, bf16[8,4,24,1280]{3,2,1,0:T(8,128)(2,1)}, u32[]{:S(2)}) copy-start(bf16[8,4,24,1280]{3,2,1,0:T(8,128)(2,1)} %get-tuple-element.15.refs_1_) | copy-start | bytes 5898244
  70.0 2.3 %copy-start.4 = (bf16[8,160,128]{2,1,0:T(8,128)(2,1)S(1)}, bf16[8,160,128]{2,1,0:T(8,128)(2,1)}, u32[]{:S(2)}) copy-start(bf16[8,160,128]{2,1,0:T(8,128)(2,1)} %get-tuple-element.18) | copy-start | bytes 983044
  73.0 1.0 copy-start.2
  75.5 49.5 %copy-start.6 = (bf16[1280,20]{0,1:T(8,128)(2,1)S(1)}, bf16[1280,20]{0,1:T(8,128)(2,1)}, u32[]{:S(2)}) copy-start(bf16[1280,20]{0,1:T(8,128)(2,1)} %param.19) | copy-start | bytes 153604
  116.6 22.6 %copy-start.5 = (bf16[128,1280]{1,0:T(8,128)(2,1)S(1)}, bf16[128,1280]{1,0:T(8,128)(2,1)}, u32[]{:S(2)}) copy-start(bf16[128,1280]{1,0:T(8,128)(2,1)} %param.15) | copy-start | bytes 983044
  119.1 19.7 %all-to-all-start = ((bf16[64,2,1408]{2,1,0:T(2,128)(2,1)}), bf16[64,2,1408]{2,1,0:T(2,128)(2,1)S(1)}, u32[]{:S(2)}, u32[]{:S(2)}) async-start(bf16[64,2,1408]{2,1,0:T(2,128)(2,1)} %reshape.116), calls=%async_computation | async-start | bytes 720896 | tf_op jit(solution)/shard_map/all_to_all | solution.py:500
  184.5 14.6 %copy-start = (bf16[8,4,24,1280]{3,2,1,0:T(8,128)(2,1)S(1)}, bf16[8,4,24,1280]{3,2,1,0:T(8,128)(2,1)}, u32[]{:S(2)}) copy-start(bf16[8,4,24,1280]{3,2,1,0:T(8,128)(2,1)} %get-tuple-element.20.refs_1_) | copy-start | bytes 5898244
  196.8 2.3 %copy-start.3 = (bf16[8,160,128]{2,1,0:T(8,128)(2,1)S(1)}, bf16[8,160,128]{2,1,0:T(8,128)(2,1)}, u32[]{:S(2)}) copy-start(bf16[8,160,128]{2,1,0:T(8,128)(2,1)} %get-tuple-element.23) | copy-start | bytes 983044

commit v3 on v2

v3 whole, which is shorter than its diff:
```python
import functools

import jax
import jax.numpy as jnp
from jax import lax
from jax.experimental import pallas as pl
from jax.experimental.pallas import tpu as pltpu
from jax.sharding import PartitionSpec as P

HEAD_DIM = 80
SEND_CAP = 2
N_TP = 8
N_Z = 8
N_X = 4
SHARD = 20
SHARD_PAD = 24
LANES = 128


EPSILON = 1e-05
MASKED = -1e30
MESH = pl.DeviceIdType.MESH


def layer_norm(rows):
    widened = rows.astype(jnp.float32)
    row_mean = jnp.mean(widened, axis=-1, keepdims=True)
    centred = widened - row_mean
    spread = jnp.mean(centred * centred, axis=-1, keepdims=True)
    return (centred * lax.rsqrt(spread + EPSILON)).astype(jnp.bfloat16)


def times_transpose(left, right):
    return lax.dot_general(
        left, right, (((1,), (1,)), ((), ())), preferred_element_type=jnp.float32
    )


def wrap(value, count):
    return lax.rem(value + count, count)


def greet(devices):
    barrier = pltpu.get_barrier_semaphore()
    for device in devices:
        pl.semaphore_signal(barrier, inc=1, device_id=device, device_id_type=MESH)
    pl.semaphore_wait(barrier, len(devices))


Q_BLOCK = 256


def attend(qv, keys, label_rows, store, causal):
    heads_here, row_count = keys.shape[:2]
    factor = HEAD_DIM ** (-0.5) * 1.4426950408889634
    key_labels = jnp.concatenate(
        [jnp.broadcast_to(label, (LANES, LANES)).T for label in label_rows], axis=0
    )
    lanes_per = Q_BLOCK // LANES
    for block in range(row_count // Q_BLOCK):
        first = block * Q_BLOCK
        targets = range(block * lanes_per, (block + 1) * lanes_per)
        end_key = first + Q_BLOCK if causal else row_count
        allowed = jnp.concatenate(
            [key_labels[:end_key] == label_rows[target] for target in targets], axis=1
        )
        if causal:
            key_ids = lax.broadcasted_iota(jnp.int32, (end_key, Q_BLOCK), 0)
            query_ids = lax.broadcasted_iota(jnp.int32, (end_key, Q_BLOCK), 1) + first
            allowed = allowed & (query_ids >= key_ids)
        for head in range(heads_here):
            here = slice(head * HEAD_DIM, (head + 1) * HEAD_DIM)
            after = (heads_here + head) * HEAD_DIM
            queries = jnp.concatenate([qv[target, here, :] for target in targets], axis=1)
            values = jnp.concatenate(
                [qv[part, after : after + HEAD_DIM, :] for part in range(end_key // LANES)],
                axis=1,
            )
            scores = jnp.dot(
                keys[head, :end_key, :], queries, preferred_element_type=jnp.float32
            )
            scores = jnp.where(allowed, scores, MASKED)
            top = jnp.max(scores, axis=0, keepdims=True)
            weights = jnp.exp2((scores - top) * factor)
            total = jnp.sum(weights, axis=0, keepdims=True)
            mixed = jnp.dot(
                values, weights.astype(jnp.bfloat16), preferred_element_type=jnp.float32
            )
            store(targets, here, (mixed / total).astype(jnp.bfloat16))
        yield targets


def layer_kernel(causal, *refs):
    own, own_label, own_shard, weights_hbm, received, shards, other = refs[:7]
    slots, labels, weights, qv, keys, heads = refs[7:13]
    row_send, row_recv, lab_send, lab_recv, z_send, z_recv = refs[13:19]
    x_send, x_recv, core_send, core_recv, head_send, head_recv, local_sem = refs[19:]
    tp = lax.axis_index("tp")
    grp = lax.axis_index("grp")
    core = lax.rem(grp, 2)
    z_here = lax.rem(grp // 2, N_Z)
    x_here = grp // (2 * N_Z)
    half = own.shape[0] // 2
    features = heads.shape[1]

    def at_xz(x, z):
        return {"grp": (x * N_Z + z) * 2 + core}

    partner = {"grp": grp + 1 - 2 * core}
    tp_next = [{"tp": wrap(tp + 1, N_TP)}, {"tp": wrap(tp - 1, N_TP)}]
    z_next = [at_xz(x_here, wrap(z_here + 1, N_Z)), at_xz(x_here, wrap(z_here - 1, N_Z))]
    x_peers = [at_xz(wrap(x_here + d, N_X), z_here) for d in range(1, N_X)]

    fetch = pltpu.make_async_copy(weights_hbm, weights, local_sem.at[0])
    fetch.start()
    own_place = shards.at[z_here, x_here]
    keep_shard = pltpu.make_async_copy(own_shard, own_place, local_sem.at[1])
    keep_shard.start()
    slots[tp] = layer_norm(own[...])
    labels[tp] = own_label[...]
    greet([{"tp": wrap(tp + d, N_TP)} for d in range(1, N_TP)] + z_next + x_peers + [partner])

    pending = []

    def send(src, dst, send_sem, recv_sem, device):
        copy = pltpu.make_async_remote_copy(
            src_ref=src,
            dst_ref=dst,
            send_sem=send_sem,
            recv_sem=recv_sem,
            device_id=device,
            device_id_type=MESH,
        )
        copy.start()
        pending.append(copy)
        return copy

    def block_of(way, step):
        return wrap(tp - step, N_TP) if way == 0 else wrap(tp + step, N_TP)

    def z_block(way, step):
        return wrap(z_here - step, N_Z) if way == 0 else wrap(z_here + step, N_Z)

    def row_copy(way, step, part):
        place = slots.at[block_of(way, step), pl.ds(part * half, half)]
        slot = (way * 4 + step) * 2 + part
        return send(place, place, row_send.at[slot], row_recv.at[slot], tp_next[way])

    def label_copy(way, step):
        place = labels.at[block_of(way, step)]
        slot = way * 4 + step
        return send(place, place, lab_send.at[slot], lab_recv.at[slot], tp_next[way])

    def shard_copy(way, step, part):
        place = shards.at[z_block(way, step), pl.ds(part * 2, 2)]
        slot = (way * 4 + step) * 2 + part
        return send(place, place, z_send.at[slot], z_recv.at[slot], z_next[way])

    core_copies = []

    def core_copy(way, step):
        block = z_block(way, step)
        slot = way * 5 + step
        core_copies.append(
            send(shards.at[block], other.at[block], core_send.at[slot], core_recv.at[slot], partner)
        )

    def project(block):
        found = lax.dot_general(
            weights[...],
            slots[block],
            (((1,), (1,)), ((), ())),
            preferred_element_type=jnp.float32,
        )
        qv[block, :features, :] = found[:features].astype(jnp.bfloat16)
        qv[block, features:, :] = found[2 * features :].astype(jnp.bfloat16)
        place = pl.ds(pl.multiple_of(block * LANES, LANES), LANES)
        for head in range(features // HEAD_DIM):
            begin = features + head * HEAD_DIM
            keys[head, place, :] = found[begin : begin + HEAD_DIM].T.astype(jnp.bfloat16)

    row_ring, label_ring, shard_ring = {}, {}, {}
    for part in range(2):
        for way in range(2):
            row_ring[way, 0, part] = row_copy(way, 0, part)
    for way in range(2):
        label_ring[way, 0] = label_copy(way, 0)
    x_copies = [
        send(own_shard, own_place, x_send.at[d], x_recv.at[d], x_peers[d]) for d in range(N_X - 1)
    ]
    fetch.wait()
    project(tp)
    keep_shard.wait()
    for copy in x_copies:
        copy.wait_recv()
    for part in range(2):
        for way in range(2):
            shard_ring[way, 0, part] = shard_copy(way, 0, part)
    core_copy(0, 0)
    for step in range(1, 4):
        for part in range(2):
            for way in range(2):
                row_ring[way, step - 1, part].wait_recv()
                if step < 3 or part == way:
                    row_ring[way, step, part] = row_copy(way, step, part)
        for way in range(2):
            label_ring[way, step - 1].wait_recv()
            if step < 3 or way == 0:
                label_ring[way, step] = label_copy(way, step)
        for part in range(2):
            for way in range(2):
                shard_ring[way, step - 1, part].wait_recv()
                if step < 3 or part == way:
                    shard_ring[way, step, part] = shard_copy(way, step, part)
        for way in range(2):
            core_copy(way, step)
        for way in range(2):
            project(block_of(way, step))
    for way in range(2):
        row_ring[way, 3, way].wait_recv()
    label_ring[0, 3].wait_recv()
    project(block_of(0, 4))
    for way in range(2):
        shard_ring[way, 3, way].wait_recv()
    core_copy(0, 4)

    def store(targets, here, mixed):
        for index, target in enumerate(targets):
            heads[target, here, :] = mixed[:, index * LANES : (index + 1) * LANES]

    def head_copy(target):
        return pltpu.make_async_remote_copy(
            src_ref=heads.at[target],
            dst_ref=received.at[tp],
            send_sem=head_send.at[target],
            recv_sem=head_recv.at[tp],
            device_id={"tp": target},
            device_id_type=MESH,
        )

    keep_heads = pltpu.make_async_copy(heads.at[tp], received.at[tp], local_sem.at[2])
    label_rows = [labels[part].astype(jnp.float32) for part in range(N_TP)]
    for targets in attend(qv, keys, label_rows, store, causal):
        for target in targets:

            @pl.when(tp != target)
            def _():
                head_copy(target).start()

    keep_heads.start()
    keep_heads.wait()
    for target in range(N_TP):

        @pl.when(tp != target)
        def _():
            arrival = pltpu.make_async_remote_copy(
                src_ref=heads.at[target],
                dst_ref=received.at[target],
                send_sem=head_send.at[target],
                recv_sem=head_recv.at[target],
                device_id={"tp": target},
                device_id_type=MESH,
            )
            arrival.wait_send()
            arrival.wait_recv()

    for copy in core_copies:
        copy.wait_recv()
    for copy in pending:
        copy.wait_send()


def run_layer(rows, labels, qkv, shard, causal, collective_id):
    row_total, width = rows.shape
    features = qkv.shape[1]
    weights = qkv.reshape(3 * features, width)
    vmem = pl.BlockSpec(memory_space=pltpu.VMEM)
    hbm = pl.BlockSpec(memory_space=pl.ANY)
    dma = pltpu.SemaphoreType.DMA
    bf16 = jnp.bfloat16
    all_shards = jax.ShapeDtypeStruct((N_Z, N_X, *shard.shape), bf16)
    return pl.pallas_call(
        functools.partial(layer_kernel, causal),
        out_shape=[
            jax.ShapeDtypeStruct((N_TP, features, row_total), bf16),
            all_shards,
            all_shards,
        ],
        in_specs=[vmem, vmem, vmem, hbm],
        out_specs=[hbm] * 3,
        scratch_shapes=[
            pltpu.VMEM((N_TP, row_total, width), bf16),
            pltpu.VMEM((N_TP, *labels.shape), labels.dtype),
            pltpu.VMEM(weights.shape, bf16),
            pltpu.VMEM((N_TP, 2 * features, row_total), bf16),
            pltpu.VMEM((features // HEAD_DIM, N_TP * row_total, HEAD_DIM), bf16),
            pltpu.VMEM((N_TP, features, row_total), bf16),
            dma((16,)),
            dma((16,)),
            dma((8,)),
            dma((8,)),
            dma((16,)),
            dma((16,)),
            dma((3,)),
            dma((3,)),
            dma((10,)),
            dma((10,)),
            dma((8,)),
            dma((8,)),
            dma((3,)),
        ],
        compiler_params=pltpu.CompilerParams(collective_id=collective_id, has_side_effects=True),
    )(rows, labels, shard, weights)


def merge_kernel(own, weights_hbm, image, slots, weights, results, *sems):
    row_send, row_recv, col_send, col_recv, local_sem = sems
    tp = lax.axis_index("tp")
    half = own.shape[0] // 2
    greet([{"tp": wrap(tp + d, N_TP)} for d in range(1, N_TP)])
    neighbours = [{"tp": wrap(tp + 1, N_TP)}, {"tp": wrap(tp - 1, N_TP)}]

    def block_of(way, step):
        return wrap(tp - step, N_TP) if way == 0 else wrap(tp + step, N_TP)

    def row_copy(way, step, part):
        span = pl.ds(part * half, half)
        dst = slots.at[block_of(way, step), span]
        slot = (way * 4 + step) * 2 + part
        return pltpu.make_async_remote_copy(
            src_ref=own.at[span] if step == 0 else dst,
            dst_ref=dst,
            send_sem=row_send.at[slot],
            recv_sem=row_recv.at[slot],
            device_id=neighbours[way],
            device_id_type=MESH,
        )

    pending = []
    ring = {}

    def start(way, step, part):
        ring[way, step, part] = row_copy(way, step, part)
        ring[way, step, part].start()
        pending.append(ring[way, step, part])

    for part in range(2):
        for way in range(2):
            start(way, 0, part)
    fetch = pltpu.make_async_copy(weights_hbm, weights, local_sem.at[0])
    fetch.start()
    fetch.wait()

    def columns(block):
        return times_transpose(block, weights[...]).astype(jnp.bfloat16)

    results[tp] = columns(own[...])
    keep = pltpu.make_async_copy(results.at[tp], image.at[tp], local_sem.at[1])
    keep.start()
    arrivals = []

    def give(way, step):
        block = block_of(way, step)
        results[block] = columns(slots[block])
        copy = pltpu.make_async_remote_copy(
            src_ref=results.at[block],
            dst_ref=image.at[tp],
            send_sem=col_send.at[way * 5 + step],
            recv_sem=col_recv.at[way * 5 + step],
            device_id={"tp": block},
            device_id_type=MESH,
        )
        copy.start()
        pending.append(copy)
        arrivals.append(copy)

    for step in range(1, 4):
        for part in range(2):
            for way in range(2):
                ring[way, step - 1, part].wait_recv()
                if step < 3 or part == way:
                    start(way, step, part)
        for way in range(2):
            give(way, step)
    for way in range(2):
        ring[way, 3, way].wait_recv()
    give(0, 4)
    keep.wait()
    for copy in arrivals:
        copy.wait_recv()
    for copy in pending:
        copy.wait_send()


def merge_rows(merged, merge_w, collective_id):
    row_total, depth = merged.shape
    features = merge_w.shape[0]
    hbm = pl.BlockSpec(memory_space=pl.ANY)
    dma = pltpu.SemaphoreType.DMA
    return pl.pallas_call(
        merge_kernel,
        out_shape=jax.ShapeDtypeStruct((N_TP, row_total, features), jnp.bfloat16),
        in_specs=[pl.BlockSpec(memory_space=pltpu.VMEM), hbm],
        out_specs=hbm,
        scratch_shapes=[
            pltpu.VMEM((N_TP, row_total, depth), jnp.bfloat16),
            pltpu.VMEM((features, depth), jnp.bfloat16),
            pltpu.VMEM((N_TP, row_total, features), jnp.bfloat16),
            dma((16,)),
            dma((16,)),
            dma((10,)),
            dma((10,)),
            dma((2,)),
        ],
        compiler_params=pltpu.CompilerParams(collective_id=collective_id, has_side_effects=True),
    )(merged, merge_w)


def attention_layer(rows, labels, qkv, columns, causal, first_id):
    shard = jnp.pad(columns.T, ((0, SHARD_PAD - SHARD), (0, 0)))
    own_heads, shards, other = run_layer(rows, labels, qkv, shard, causal, first_id)
    own_heads = own_heads.reshape(rows.shape[1], rows.shape[0])

    def project(part):
        flat = part.reshape(N_Z * N_X * SHARD_PAD, rows.shape[1])
        return jnp.dot(flat, own_heads, preferred_element_type=jnp.float32)

    here, there = project(shards), project(other)
    first = lax.rem(lax.axis_index("grp"), 2) == 0
    both = jnp.stack([jnp.where(first, here, there), jnp.where(first, there, here)])
    both = both.reshape(2, N_Z, N_X, SHARD_PAD, rows.shape[0])[:, :, :, :SHARD]
    projected = both.transpose(4, 2, 1, 0, 3).reshape(rows.shape)
    return (rows.astype(jnp.float32) + projected).astype(jnp.bfloat16)


def per_device(
    patches, pictures, vis_qkv, vis_out, merge_w, text, places, segments, txt_qkv, txt_out
):
    tp_count = lax.axis_size("tp")
    grp_count = lax.axis_size("grp")
    width = patches.shape[1]
    vis_hidden = attention_layer(patches, pictures, vis_qkv, vis_out, False, 0)
    merged = layer_norm(vis_hidden).reshape(patches.shape[0] // 4, 4 * width)
    row_total = places.shape[0]
    image_parts = merge_rows(merged, merge_w, 2)
    image_rows = image_parts.transpose(1, 0, 2).reshape(row_total, width)
    tok_count = text.shape[0]
    group_tokens = tok_count * tp_count
    dest_group = places // group_tokens
    dest_local = places % tok_count
    row_ids = jnp.arange(row_total, dtype=jnp.int32)
    earlier = row_ids[:, None] > row_ids[None, :]
    same_dest = dest_group[:, None] == dest_group[None, :]
    slot_rank = jnp.sum((earlier & same_dest).astype(jnp.int32), axis=1)
    slot_index = dest_group * SEND_CAP + slot_rank
    slot_ids = jnp.arange(grp_count * SEND_CAP, dtype=jnp.int32)
    slot_pick = (slot_ids[:, None] == slot_index[None, :]).astype(jnp.bfloat16)
    marks = jnp.broadcast_to((dest_local + 1)[:, None], (row_total, LANES)).astype(jnp.bfloat16)
    send_rows = jnp.dot(
        slot_pick,
        jnp.concatenate([image_rows, marks], axis=1),
        preferred_element_type=jnp.float32,
    ).astype(jnp.bfloat16)
    send_rows = send_rows.reshape(grp_count, SEND_CAP, width + LANES)
    recv = lax.all_to_all(send_rows, "grp", split_axis=0, concat_axis=0, tiled=True)
    recv = recv.reshape(grp_count * SEND_CAP, width + LANES)
    recv_rows = recv[:, :width]
    recv_pos = recv[:, width].astype(jnp.int32) - 1
    position_hit = jnp.arange(tok_count, dtype=jnp.int32)[:, None] == recv_pos[None, :]
    placed = jnp.dot(
        position_hit.astype(jnp.bfloat16), recv_rows, preferred_element_type=jnp.float32
    ).astype(jnp.bfloat16)
    covered = jnp.any(position_hit, axis=1)
    prompt = jnp.where(covered[:, None], placed, text)
    return attention_layer(prompt, segments, txt_qkv, txt_out, True, 4)


def solution(mesh):
    placed = (
        P(("grp", "tp"), None),
        P("grp", "tp"),
        P(None, "tp", None),
        P(None, "grp"),
        P("tp", None),
        P(("grp", "tp"), None),
        P(("grp", "tp")),
        P("grp", "tp"),
        P(None, "tp", None),
        P(None, "grp"),
    )
    return jax.shard_map(
        per_device, mesh=mesh, in_specs=placed, out_specs=P(("grp", "tp"), None), check_vma=False
    )
```

time: 203 us -> 181 us (0.89)
  Pallas kernels: 161 us -> 144 us
  other arithmetic: 7.95 us -> 1.79 us
    pallas_call x6 -> x2, Pallas kernels: 120 us -> 104 us  [run_layer(): pl.pallas_call(functools.partial(layer_kernel, causal), out_shape=[jax.Sh...]
    convert_element_type x3 -> x1, other arithmetic: 3 us -> 0.09 us  [layer_norm(): return (centred * lax.rsqrt(spread + EPSILON)).astype(jnp.bfloat16)]
where the time goes in v3:
time: 181 us
  Pallas kernels  144 us (80%)
  waiting for transfers between devices  13.2 us (7%)
  local copies, waits for them, and re-layouts  7.63 us (4%)
  matrix products  7.33 us (4%)
  starting transfers between devices  6.57 us (4%)
    pallas_call x2, Pallas kernels, run_layer(): pl.pallas_call(functools.partial(layer_kernel, causal), out_shape=[jax.Sh...  104 us
    pallas_call x1, Pallas kernels, merge_rows(): pl.pallas_call(merge_kernel, out_shape=jax.ShapeDtypeStruct((N_TP, row_to...  40.2 us
    all_to_all x1, waiting for transfers between devices, per_device(): lax.all_to_all(send_rows, 'grp', split_axis=0, concat_axis=0, tiled=True)  13.2 us
    all_to_all x1, starting transfers between devices, per_device(): lax.all_to_all(send_rows, 'grp', split_axis=0, concat_axis=0, tiled=True)  6.57 us
    dot_general x4, matrix products, project(): return jnp.dot(flat, own_heads, preferred_element_type=jnp.float32)  6.12 us
  transfers between devices with their start and end apart: 1, of which 1 were waited for; matrix products, arithmetic and copies ran while one was open for 0% of the time, Pallas kernels for 0%

profile of v3, /device:TPU:56, one launch (start us, length us, event | category | flops | bytes accessed | tf_op | source)
XLA Modules:
  0.0 180.8 jit_solution(17893261525508229042)
XLA Ops:
  0.0 1.2 copy.31
  1.2 1.5 pad.7.refs_2_
  2.6 55.3 %shard_map.100 = (bf16[8,160,128]{2,1,0:T(8,128)(2,1)}, bf16[8,4,24,1280]{3,2,1,0:T(8,128)(2,1)}, bf16[8,4,24,1280]{3,2,1,0:T(8,128)(2,1)}) custom-call(bf16[128,1280]{1,0:T(8,128)(2,1)} %refs_0_.1, s32[1,128]{1,0:T(1,128)} %refs_1_.2, bf16[24,1280]{1,0:T(8,128)(2,1)} %pad.7.refs_2_, bf16[480,1280]{1,0:T(8,128)(2,1)} %bitcast.43), custom_call_target="tpu_custom_call" | custom-call | tf_op jit(solution)/shard_map/pallas_call | solution.py:282
  58.0 0.0 copy-start.2
  58.0 0.0 copy-start.4
  58.0 2.4 %fusion.16 = f32[768,128]{1,0:T(8,128)S(1)} fusion(bf16[768,1280]{1,0:T(8,128)(2,1)} %bitcast.33, bf16[1280,128]{1,0:T(8,128)(2,1)} %bitcast.41), kind=kOutput, calls=%fused_computation.44 | convolution fusion | flops 251658240 | bytes 2686976 | tf_op jit(solution)/shard_map/dot_general | solution.py:426
  60.4 0.0 copy-done.2
  60.4 0.0 copy-done.4
  60.4 0.7 broadcast_select_fusion.3
  61.1 0.1 copy_bitcast_fusion.1
  61.2 0.1 reshape.82
  61.2 0.2 convert_reduce_fusion
  61.4 0.2 fusion.3
  61.6 0.1 fusion.4
  61.7 0.0 copy-start.7
  61.7 0.2 copy.34
  61.9 0.9 reshape.83.own
  62.9 40.2 %shard_map.101 = bf16[8,32,160]{2,1,0:T(8,128)(2,1)} custom-call(bf16[32,5120]{1,0:T(8,128)(2,1)} %reshape.83.own, bf16[160,5120]{1,0:T(8,128)(2,1)} %weights_hbm.1), custom_call_target="tpu_custom_call" | custom-call | tf_op jit(solution)/shard_map/pallas_call | solution.py:400
  103.1 0.0 copy-start.5
  103.1 1.0 copy.35
  104.1 0.2 reshape.84
  104.3 0.0 copy-done.7
  104.3 0.2 convert_reduce_fusion.1
  104.5 0.1 broadcast_in_dim.7
  104.6 0.2 convolution_convert_fusion.1
  104.8 0.9 reshape.85
  105.7 6.6 %all-to-all-start = ((bf16[64,2,1408]{2,1,0:T(2,128)(2,1)}), bf16[64,2,1408]{2,1,0:T(2,128)(2,1)S(1)}, u32[]{:S(2)}, u32[]{:S(2)}) async-start(bf16[64,2,1408]{2,1,0:T(2,128)(2,1)} %reshape.85), calls=%async_computation | async-start | bytes 720896 | tf_op jit(solution)/shard_map/all_to_all | solution.py:465
  112.3 0.0 copy-done.6
  112.3 0.6 pad.8.refs_2_
  112.9 13.2 %all-to-all-done = bf16[64,2,1408]{2,1,0:T(2,128)(2,1)S(1)} async-done(((bf16[64,2,1408]{2,1,0:T(2,128)(2,1)}), bf16[64,2,1408]{2,1,0:T(2,128)(2,1)S(1)}, u32[]{:S(2)}, u32[]{:S(2)}) %all-to-all-start) | async-done | bytes 360480 | tf_op jit(solution)/shard_map/all_to_all | solution.py:465
  126.1 0.1 reshape.86
  126.3 0.1 add_reduce_fusion
  126.4 0.1 fusion.9
  126.5 0.0 copy-done.5
  126.5 1.0 fusion.refs_0_
  127.5 48.4 %shard_map.102 = (bf16[8,160,128]{2,1,0:T(8,128)(2,1)}, bf16[8,4,24,1280]{3,2,1,0:T(8,128)(2,1)}, bf16[8,4,24,1280]{3,2,1,0:T(8,128)(2,1)}) custom-call(bf16[128,1280]{1,0:T(8,128)(2,1)} %fusion.refs_0_, s32[1,128]{1,0:T(1,128)} %refs_1_.3, bf16[24,1280]{1,0:T(8,128)(2,1)} %pad.8.refs_2_, bf16[480,1280]{1,0:T(8,128)(2,1)} %bitcast.44), custom_call_target="tpu_custom_call" | custom-call | tf_op jit(solution)/shard_map/pallas_call | solution.py:282
  175.9 0.0 copy-start.1
  175.9 0.0 copy-start.3
  175.9 2.4 %fusion.17 = f32[768,128]{1,0:T(8,128)S(1)} fusion(bf16[768,1280]{1,0:T(8,128)(2,1)} %bitcast.34, bf16[1280,128]{1,0:T(8,128)(2,1)} %bitcast.39), kind=kOutput, calls=%fused_computation.45 | convolution fusion | flops 251658240 | bytes 2686976 | tf_op jit(solution)/shard_map/dot_general | solution.py:426
  178.3 0.0 copy-done.1
  178.3 0.0 copy-done.3
  178.3 0.7 broadcast_select_fusion.1
  179.0 0.0 copy-start
  179.0 0.1 copy_bitcast_fusion
  179.1 0.1 reshape.91
  179.2 0.2 copy.38
  179.4 0.6 copy-done
  180.0 0.8 add_convert_fusion
  (5 shorter events, 0.0 us)
Async XLA Ops:
  58.0 2.4 %copy-start.2 = (bf16[8,4,24,1280]{3,2,1,0:T(8,128)(2,1)S(1)}, bf16[8,4,24,1280]{3,2,1,0:T(8,128)(2,1)}, u32[]{:S(2)}) copy-start(bf16[8,4,24,1280]{3,2,1,0:T(8,128)(2,1)} %get-tuple-element.11) | copy-start | bytes 5898244
  58.0 2.4 %copy-start.4 = (bf16[8,160,128]{2,1,0:T(8,128)(2,1)S(1)}, bf16[8,160,128]{2,1,0:T(8,128)(2,1)}, u32[]{:S(2)}) copy-start(bf16[8,160,128]{2,1,0:T(8,128)(2,1)} %get-tuple-element.12) | copy-start | bytes 983044
  61.7 42.6 %copy-start.7 = (s32[32]{0:T(128)S(1)}, s32[32]{0:T(128)}, u32[]{:S(2)}) copy-start(s32[32]{0:T(128)} %param.16) | copy-start | bytes 388
  62.8 49.4 %copy-start.6 = (bf16[1280,20]{0,1:T(8,128)(2,1)S(1)}, bf16[1280,20]{0,1:T(8,128)(2,1)}, u32[]{:S(2)}) copy-start(bf16[1280,20]{0,1:T(8,128)(2,1)} %param.19) | copy-start | bytes 153604
  103.1 23.4 %copy-start.5 = (bf16[128,1280]{1,0:T(8,128)(2,1)S(1)}, bf16[128,1280]{1,0:T(8,128)(2,1)}, u32[]{:S(2)}) copy-start(bf16[128,1280]{1,0:T(8,128)(2,1)} %param.15) | copy-start | bytes 983044
  105.7 20.4 %all-to-all-start = ((bf16[64,2,1408]{2,1,0:T(2,128)(2,1)}), bf16[64,2,1408]{2,1,0:T(2,128)(2,1)S(1)}, u32[]{:S(2)}, u32[]{:S(2)}) async-start(bf16[64,2,1408]{2,1,0:T(2,128)(2,1)} %reshape.85), calls=%async_computation | async-start | bytes 720896 | tf_op jit(solution)/shard_map/all_to_all | solution.py:465
  175.9 2.4 %copy-start.1 = (bf16[8,4,24,1280]{3,2,1,0:T(8,128)(2,1)S(1)}, bf16[8,4,24,1280]{3,2,1,0:T(8,128)(2,1)}, u32[]{:S(2)}) copy-start(bf16[8,4,24,1280]{3,2,1,0:T(8,128)(2,1)} %get-tuple-element.14) | copy-start | bytes 5898244
  175.9 2.4 %copy-start.3 = (bf16[8,160,128]{2,1,0:T(8,128)(2,1)S(1)}, bf16[8,160,128]{2,1,0:T(8,128)(2,1)}, u32[]{:S(2)}) copy-start(bf16[8,160,128]{2,1,0:T(8,128)(2,1)} %get-tuple-element.15) | copy-start | bytes 983044
  179.0 1.0 copy-start

commit v4 on v3

--- a/solution.py
+++ b/solution.py
@@ -91,10 +91,10 @@
 
 
 def layer_kernel(causal, *refs):
-    own, own_label, own_shard, weights_hbm, received, shards, other = refs[:7]
-    slots, labels, weights, qv, keys, heads = refs[7:13]
-    row_send, row_recv, lab_send, lab_recv, z_send, z_recv = refs[13:19]
-    x_send, x_recv, core_send, core_recv, head_send, head_recv, local_sem = refs[19:]
+    own, own_label, columns, weights_hbm, received, shards, other = refs[:7]
+    slots, labels, weights, qv, keys, heads, own_shard = refs[7:14]
+    row_send, row_recv, lab_send, lab_recv, z_send, z_recv = refs[14:20]
+    x_send, x_recv, core_send, core_recv, head_send, head_recv, local_sem = refs[20:]
     tp = lax.axis_index("tp")
     grp = lax.axis_index("grp")
     core = lax.rem(grp, 2)
@@ -114,8 +114,8 @@
     fetch = pltpu.make_async_copy(weights_hbm, weights, local_sem.at[0])
     fetch.start()
     own_place = shards.at[z_here, x_here]
-    keep_shard = pltpu.make_async_copy(own_shard, own_place, local_sem.at[1])
-    keep_shard.start()
+    own_shard[...] = jnp.zeros_like(own_shard)
+    own_shard[: columns.shape[0], :] = columns[...]
     slots[tp] = layer_norm(own[...])
     labels[tp] = own_label[...]
     greet([{"tp": wrap(tp + d, N_TP)} for d in range(1, N_TP)] + z_next + x_peers + [partner])
@@ -188,15 +188,25 @@
     x_copies = [
         send(own_shard, own_place, x_send.at[d], x_recv.at[d], x_peers[d]) for d in range(N_X - 1)
     ]
+    keep_shard = pltpu.make_async_copy(own_shard, own_place, local_sem.at[1])
+    keep_shard.start()
     fetch.wait()
     project(tp)
-    keep_shard.wait()
-    for copy in x_copies:
-        copy.wait_recv()
-    for part in range(2):
-        for way in range(2):
-            shard_ring[way, 0, part] = shard_copy(way, 0, part)
-    core_copy(0, 0)
+
+    def shard_step(step):
+        if step == 0:
+            keep_shard.wait()
+            for copy in x_copies:
+                copy.wait_recv()
+        for part in range(2):
+            for way in range(2):
+                if step and (step < 4 or part == way):
+                    shard_ring[way, step - 1, part].wait_recv()
+                if step < 3 or (step == 3 and part == way):
+                    shard_ring[way, step, part] = shard_copy(way, step, part)
+        for way in range(2 if step in (1, 2, 3) else 1):
+            core_copy(way, step)
+
     for step in range(1, 4):
         for part in range(2):
             for way in range(2):
@@ -207,23 +217,13 @@
             label_ring[way, step - 1].wait_recv()
             if step < 3 or way == 0:
                 label_ring[way, step] = label_copy(way, step)
-        for part in range(2):
-            for way in range(2):
-                shard_ring[way, step - 1, part].wait_recv()
-                if step < 3 or part == way:
-                    shard_ring[way, step, part] = shard_copy(way, step, part)
-        for way in range(2):
-            core_copy(way, step)
         for way in range(2):
             project(block_of(way, step))
+        shard_step(step - 1)
     for way in range(2):
         row_ring[way, 3, way].wait_recv()
     label_ring[0, 3].wait_recv()
     project(block_of(0, 4))
-    for way in range(2):
-        shard_ring[way, 3, way].wait_recv()
-    core_copy(0, 4)
-
     def store(targets, here, mixed):
         for index, target in enumerate(targets):
             heads[target, here, :] = mixed[:, index * LANES : (index + 1) * LANES]
@@ -240,7 +240,9 @@
 
     keep_heads = pltpu.make_async_copy(heads.at[tp], received.at[tp], local_sem.at[2])
     label_rows = [labels[part].astype(jnp.float32) for part in range(N_TP)]
-    for targets in attend(qv, keys, label_rows, store, causal):
+    for done, targets in enumerate(attend(qv, keys, label_rows, store, causal)):
+        if done < 2:
+            shard_step(3 + done)
         for target in targets:
 
             @pl.when(tp != target)
@@ -278,7 +280,7 @@
     hbm = pl.BlockSpec(memory_space=pl.ANY)
     dma = pltpu.SemaphoreType.DMA
     bf16 = jnp.bfloat16
-    all_shards = jax.ShapeDtypeStruct((N_Z, N_X, *shard.shape), bf16)
+    all_shards = jax.ShapeDtypeStruct((N_Z, N_X, SHARD_PAD, width), bf16)
     return pl.pallas_call(
         functools.partial(layer_kernel, causal),
         out_shape=[
@@ -295,6 +297,7 @@
             pltpu.VMEM((N_TP, 2 * features, row_total), bf16),
             pltpu.VMEM((features // HEAD_DIM, N_TP * row_total, HEAD_DIM), bf16),
             pltpu.VMEM((N_TP, features, row_total), bf16),
+            pltpu.VMEM((SHARD_PAD, width), bf16),
             dma((16,)),
             dma((16,)),
             dma((8,)),
@@ -313,7 +316,7 @@
     )(rows, labels, shard, weights)
 
 
-def merge_kernel(own, weights_hbm, image, slots, weights, results, *sems):
+def merge_kernel(own, weights_hbm, out, slots, weights, results, image, *sems):
     row_send, row_recv, col_send, col_recv, local_sem = sems
     tp = lax.axis_index("tp")
     half = own.shape[0] // 2
@@ -388,6 +391,9 @@
     keep.wait()
     for copy in arrivals:
         copy.wait_recv()
+    out[...] = jnp.concatenate(
+        [image[part].astype(jnp.float32) for part in range(N_TP)], axis=1
+    ).astype(jnp.bfloat16)
     for copy in pending:
         copy.wait_send()
 
@@ -399,12 +405,13 @@
     dma = pltpu.SemaphoreType.DMA
     return pl.pallas_call(
         merge_kernel,
-        out_shape=jax.ShapeDtypeStruct((N_TP, row_total, features), jnp.bfloat16),
+        out_shape=jax.ShapeDtypeStruct((row_total, N_TP * features), jnp.bfloat16),
         in_specs=[pl.BlockSpec(memory_space=pltpu.VMEM), hbm],
-        out_specs=hbm,
+        out_specs=pl.BlockSpec(memory_space=pltpu.VMEM),
         scratch_shapes=[
             pltpu.VMEM((N_TP, row_total, depth), jnp.bfloat16),
             pltpu.VMEM((features, depth), jnp.bfloat16),
+            pltpu.VMEM((N_TP, row_total, features), jnp.bfloat16),
             pltpu.VMEM((N_TP, row_total, features), jnp.bfloat16),
             dma((16,)),
             dma((16,)),
@@ -417,8 +424,7 @@
 
 
 def attention_layer(rows, labels, qkv, columns, causal, first_id):
-    shard = jnp.pad(columns.T, ((0, SHARD_PAD - SHARD), (0, 0)))
-    own_heads, shards, other = run_layer(rows, labels, qkv, shard, causal, first_id)
+    own_heads, shards, other = run_layer(rows, labels, qkv, columns.T, causal, first_id)
     own_heads = own_heads.reshape(rows.shape[1], rows.shape[0])
 
     def project(part):
@@ -442,8 +448,7 @@
     vis_hidden = attention_layer(patches, pictures, vis_qkv, vis_out, False, 0)
     merged = layer_norm(vis_hidden).reshape(patches.shape[0] // 4, 4 * width)
     row_total = places.shape[0]
-    image_parts = merge_rows(merged, merge_w, 2)
-    image_rows = image_parts.transpose(1, 0, 2).reshape(row_total, width)
+    image_rows = merge_rows(merged, merge_w, 2)
     tok_count = text.shape[0]
     group_tokens = tok_count * tp_count
     dest_group = places // group_tokens

time: 181 us -> 183 us (1.011)
  blocking collectives: 0 us -> 20 us
  waiting for transfers between devices: 13.2 us -> 0 us
  starting transfers between devices: 6.57 us -> 0 us
  Pallas kernels: 144 us -> 149 us
  local copies, waits for them, and re-layouts: 7.63 us -> 3.61 us
    all_to_all x0 -> x1, blocking collectives: none -> 20 us  [per_device(): lax.all_to_all(send_rows, 'grp', split_axis=0, concat_axis=0, tiled=True)]
    all_to_all x1 -> x0, waiting for transfers between devices: 13.2 us -> none  [per_device(): lax.all_to_all(send_rows, 'grp', split_axis=0, concat_axis=0, tiled=True)]
    all_to_all x1 -> x0, starting transfers between devices: 6.57 us -> none  [per_device(): lax.all_to_all(send_rows, 'grp', split_axis=0, concat_axis=0, tiled=True)]
    pallas_call x2, Pallas kernels: 104 us -> 109 us  [run_layer(): pl.pallas_call(functools.partial(layer_kernel, causal), out_shape=[jax.Sh...]
    pad x2 -> x0, local copies, waits for them, and re-layouts: 2.09 us -> none  [attention_layer(): shard = jnp.pad(columns.T, ((0, SHARD_PAD - SHARD), (0, 0)))]
  transfers between devices with their start and end apart: 1 -> 0, of which waited for: 1 -> 0; matrix products, arithmetic and copies ran while one was open for 0% -> 0% of each run, Pallas kernels for 0% -> 0%
where the time goes in v4:
time: 183 us
  Pallas kernels  149 us (81%)
  blocking collectives  20 us (11%)
  matrix products  8.2 us (4%)
  local copies, waits for them, and re-layouts  3.61 us (2%)
    pallas_call x2, Pallas kernels, run_layer(): pl.pallas_call(functools.partial(layer_kernel, causal), out_shape=[jax.Sh...  109 us
    pallas_call x1, Pallas kernels, merge_rows(): pl.pallas_call(merge_kernel, out_shape=jax.ShapeDtypeStruct((row_total, N...  40 us
    all_to_all x1, blocking collectives, per_device(): lax.all_to_all(send_rows, 'grp', split_axis=0, concat_axis=0, tiled=True)  20 us
    dot_general x4, matrix products, project(): return jnp.dot(flat, own_heads, preferred_element_type=jnp.float32)  6.12 us

profile of v4, /device:TPU:56, one launch (start us, length us, event | category | flops | bytes accessed | tf_op | source)
XLA Modules:
  0.0 182.7 jit_solution(16149501609175444003)
XLA Ops:
  0.0 1.2 copy.29
  1.2 58.5 %shard_map.100 = (bf16[8,160,128]{2,1,0:T(8,128)(2,1)}, bf16[8,4,24,1280]{3,2,1,0:T(8,128)(2,1)}, bf16[8,4,24,1280]{3,2,1,0:T(8,128)(2,1)}) custom-call(bf16[128,1280]{1,0:T(8,128)(2,1)} %refs_0_.1, s32[1,128]{1,0:T(1,128)} %refs_1_.2, bf16[20,1280]{1,0:T(8,128)(2,1)} %bitcast.44, bf16[480,1280]{1,0:T(8,128)(2,1)} %bitcast.42), custom_call_target="tpu_custom_call" | custom-call | tf_op jit(solution)/shard_map/pallas_call | solution.py:284
  59.7 0.0 copy-start.2
  59.7 0.0 copy-start.4
  59.7 2.4 %fusion.16 = f32[768,128]{1,0:T(8,128)S(1)} fusion(bf16[768,1280]{1,0:T(8,128)(2,1)} %bitcast.32, bf16[1280,128]{1,0:T(8,128)(2,1)} %bitcast.40), kind=kOutput, calls=%fused_computation.44 | convolution fusion | flops 251658240 | bytes 2686976 | tf_op jit(solution)/shard_map/dot_general | solution.py:432
  62.1 0.0 copy-done.2
  62.1 0.0 copy-done.4
  62.1 0.7 broadcast_select_fusion.3
  62.8 0.1 copy_bitcast_fusion.1
  62.9 0.1 reshape.79
  62.9 0.0 copy-start.6
  62.9 0.2 convert_reduce_fusion
  63.1 0.2 fusion.3
  63.3 0.1 fusion.4
  63.4 0.2 copy.32
  63.6 0.9 reshape.80.own
  64.5 0.0 copy-done.6
  64.6 0.2 convert_reduce_fusion.1
  64.7 0.0 copy-start.5
  64.8 40.0 %shard_map.101 = bf16[32,1280]{1,0:T(8,128)(2,1)} custom-call(bf16[32,5120]{1,0:T(8,128)(2,1)} %reshape.80.own, bf16[160,5120]{1,0:T(8,128)(2,1)} %weights_hbm.1), custom_call_target="tpu_custom_call" | custom-call | tf_op jit(solution)/shard_map/pallas_call | solution.py:406
  104.7 0.1 broadcast_in_dim.7
  104.8 1.1 convolution_convert_fusion.1
  105.9 0.1 reshape.81
  106.1 20.0 %all_to_all.5 = bf16[64,2,1408]{2,1,0:T(2,128)(2,1)S(1)} all-to-all(bf16[64,2,1408]{2,1,0:T(2,128)(2,1)S(1)} %reshape.81), channel_id=1, replica_groups=mesh['grp'=64,'tp'=8] {'grp'}, dimensions={0} | all-to-all | bytes 720896 | tf_op jit(solution)/shard_map/all_to_all | solution.py:470
  126.0 0.1 reshape.82
  126.2 0.1 add_reduce_fusion
  126.3 0.1 fusion.9
  126.4 0.0 copy-done.5
  126.4 1.0 fusion.refs_0_
  127.4 50.4 %shard_map.102 = (bf16[8,160,128]{2,1,0:T(8,128)(2,1)}, bf16[8,4,24,1280]{3,2,1,0:T(8,128)(2,1)}, bf16[8,4,24,1280]{3,2,1,0:T(8,128)(2,1)}) custom-call(bf16[128,1280]{1,0:T(8,128)(2,1)} %fusion.refs_0_, s32[1,128]{1,0:T(1,128)} %refs_1_.3, bf16[20,1280]{1,0:T(8,128)(2,1)} %bitcast.45, bf16[480,1280]{1,0:T(8,128)(2,1)} %bitcast.43), custom_call_target="tpu_custom_call" | custom-call | tf_op jit(solution)/shard_map/pallas_call | solution.py:284
  177.8 0.0 copy-start.1
  177.8 0.0 copy-start.3
  177.8 2.4 %fusion.17 = f32[768,128]{1,0:T(8,128)S(1)} fusion(bf16[768,1280]{1,0:T(8,128)(2,1)} %bitcast.33, bf16[1280,128]{1,0:T(8,128)(2,1)} %bitcast.38), kind=kOutput, calls=%fused_computation.45 | convolution fusion | flops 251658240 | bytes 2686976 | tf_op jit(solution)/shard_map/dot_general | solution.py:432
  180.2 0.0 copy-done.1
  180.2 0.0 copy-done.3
  180.2 0.7 broadcast_select_fusion.1
  180.9 0.0 copy-start
  180.9 0.1 copy_bitcast_fusion
  181.0 0.1 reshape.87
  181.0 0.2 copy.35
  181.3 0.6 copy-done
  181.9 0.8 add_convert_fusion
  (4 shorter events, 0.0 us)
Async XLA Ops:
  59.7 2.4 %copy-start.2 = (bf16[8,4,24,1280]{3,2,1,0:T(8,128)(2,1)S(1)}, bf16[8,4,24,1280]{3,2,1,0:T(8,128)(2,1)}, u32[]{:S(2)}) copy-start(bf16[8,4,24,1280]{3,2,1,0:T(8,128)(2,1)} %get-tuple-element.11) | copy-start | bytes 5898244
  59.7 2.4 %copy-start.4 = (bf16[8,160,128]{2,1,0:T(8,128)(2,1)S(1)}, bf16[8,160,128]{2,1,0:T(8,128)(2,1)}, u32[]{:S(2)}) copy-start(bf16[8,160,128]{2,1,0:T(8,128)(2,1)} %get-tuple-element.12) | copy-start | bytes 983044
  62.9 1.6 copy-start.6
  64.7 61.7 %copy-start.5 = (bf16[128,1280]{1,0:T(8,128)(2,1)S(1)}, bf16[128,1280]{1,0:T(8,128)(2,1)}, u32[]{:S(2)}) copy-start(bf16[128,1280]{1,0:T(8,128)(2,1)} %param.15) | copy-start | bytes 983044
  177.8 2.4 %copy-start.1 = (bf16[8,4,24,1280]{3,2,1,0:T(8,128)(2,1)S(1)}, bf16[8,4,24,1280]{3,2,1,0:T(8,128)(2,1)}, u32[]{:S(2)}) copy-start(bf16[8,4,24,1280]{3,2,1,0:T(8,128)(2,1)} %get-tuple-element.14) | copy-start | bytes 5898244
  177.8 2.4 %copy-start.3 = (bf16[8,160,128]{2,1,0:T(8,128)(2,1)S(1)}, bf16[8,160,128]{2,1,0:T(8,128)(2,1)}, u32[]{:S(2)}) copy-start(bf16[8,160,128]{2,1,0:T(8,128)(2,1)} %get-tuple-element.15) | copy-start | bytes 983044
  180.9 1.0 copy-start

commit v5 on v4

--- a/solution.py
+++ b/solution.py
@@ -207,6 +207,7 @@
         for way in range(2 if step in (1, 2, 3) else 1):
             core_copy(way, step)
 
+    shard_step(0)
     for step in range(1, 4):
         for part in range(2):
             for way in range(2):
@@ -219,11 +220,12 @@
                 label_ring[way, step] = label_copy(way, step)
         for way in range(2):
             project(block_of(way, step))
-        shard_step(step - 1)
+        shard_step(step)
     for way in range(2):
         row_ring[way, 3, way].wait_recv()
     label_ring[0, 3].wait_recv()
     project(block_of(0, 4))
+    shard_step(4)
     def store(targets, here, mixed):
         for index, target in enumerate(targets):
             heads[target, here, :] = mixed[:, index * LANES : (index + 1) * LANES]
@@ -240,9 +242,7 @@
 
     keep_heads = pltpu.make_async_copy(heads.at[tp], received.at[tp], local_sem.at[2])
     label_rows = [labels[part].astype(jnp.float32) for part in range(N_TP)]
-    for done, targets in enumerate(attend(qv, keys, label_rows, store, causal)):
-        if done < 2:
-            shard_step(3 + done)
+    for targets in attend(qv, keys, label_rows, store, causal):
         for target in targets:
 
             @pl.when(tp != target)

time: 183 us -> 177 us (0.967)
  Pallas kernels: 149 us -> 143 us
    pallas_call x2, Pallas kernels: 109 us -> 102 us  [run_layer(): pl.pallas_call(functools.partial(layer_kernel, causal), out_shape=[jax.Sh...]
where the time goes in v5:
time: 177 us; the launch traced here: 176 us
  Pallas kernels  143 us (81%)
  blocking collectives  18.8 us (11%)
  matrix products  8.2 us (5%)
  local copies, waits for them, and re-layouts  3.61 us (2%)
  other arithmetic  1.79 us (1%)
    pallas_call x2, Pallas kernels, run_layer(): pl.pallas_call(functools.partial(layer_kernel, causal), out_shape=[jax.Sh...  102 us
    pallas_call x1, Pallas kernels, merge_rows(): pl.pallas_call(merge_kernel, out_shape=jax.ShapeDtypeStruct((row_total, N...  41.5 us
    all_to_all x1, blocking collectives, per_device(): lax.all_to_all(send_rows, 'grp', split_axis=0, concat_axis=0, tiled=True)  18.8 us
    dot_general x4, matrix products, project(): return jnp.dot(flat, own_heads, preferred_element_type=jnp.float32)  6.12 us

profile of v5, /device:TPU:56, one launch (start us, length us, event | category | flops | bytes accessed | tf_op | source)
XLA Modules:
  0.0 176.1 jit_solution(7838208230696877483)
XLA Ops:
  0.0 1.2 copy.29
  1.2 55.7 %shard_map.100 = (bf16[8,160,128]{2,1,0:T(8,128)(2,1)}, bf16[8,4,24,1280]{3,2,1,0:T(8,128)(2,1)}, bf16[8,4,24,1280]{3,2,1,0:T(8,128)(2,1)}) custom-call(bf16[128,1280]{1,0:T(8,128)(2,1)} %refs_0_.1, s32[1,128]{1,0:T(1,128)} %refs_1_.2, bf16[20,1280]{1,0:T(8,128)(2,1)} %bitcast.44, bf16[480,1280]{1,0:T(8,128)(2,1)} %bitcast.42), custom_call_target="tpu_custom_call" | custom-call | tf_op jit(solution)/shard_map/pallas_call | solution.py:284
  56.9 0.0 copy-start.2
  56.9 0.0 copy-start.4
  56.9 2.4 %fusion.16 = f32[768,128]{1,0:T(8,128)S(1)} fusion(bf16[768,1280]{1,0:T(8,128)(2,1)} %bitcast.32, bf16[1280,128]{1,0:T(8,128)(2,1)} %bitcast.40), kind=kOutput, calls=%fused_computation.44 | convolution fusion | flops 251658240 | bytes 2686976 | tf_op jit(solution)/shard_map/dot_general | solution.py:432
  59.3 0.0 copy-done.2
  59.3 0.0 copy-done.4
  59.3 0.7 broadcast_select_fusion.3
  60.0 0.1 copy_bitcast_fusion.1
  60.1 0.1 reshape.79
  60.1 0.0 copy-start.6
  60.2 0.2 convert_reduce_fusion
  60.4 0.2 fusion.3
  60.6 0.1 fusion.4
  60.6 0.2 copy.32
  60.8 0.9 reshape.80.own
  61.8 0.0 copy-done.6
  61.8 0.2 convert_reduce_fusion.1
  62.0 0.0 copy-start.5
  62.0 41.5 %shard_map.101 = bf16[32,1280]{1,0:T(8,128)(2,1)} custom-call(bf16[32,5120]{1,0:T(8,128)(2,1)} %reshape.80.own, bf16[160,5120]{1,0:T(8,128)(2,1)} %weights_hbm.1), custom_call_target="tpu_custom_call" | custom-call | tf_op jit(solution)/shard_map/pallas_call | solution.py:406
  103.5 0.1 broadcast_in_dim.7
  103.5 1.1 convolution_convert_fusion.1
  104.6 0.1 reshape.81
  104.8 18.8 %all_to_all.5 = bf16[64,2,1408]{2,1,0:T(2,128)(2,1)S(1)} all-to-all(bf16[64,2,1408]{2,1,0:T(2,128)(2,1)S(1)} %reshape.81), channel_id=1, replica_groups=mesh['grp'=64,'tp'=8] {'grp'}, dimensions={0} | all-to-all | bytes 720896 | tf_op jit(solution)/shard_map/all_to_all | solution.py:470
  123.6 0.1 reshape.82
  123.7 0.1 add_reduce_fusion
  123.8 0.1 fusion.9
  124.0 0.0 copy-done.5
  124.0 1.0 fusion.refs_0_
  125.0 46.3 %shard_map.102 = (bf16[8,160,128]{2,1,0:T(8,128)(2,1)}, bf16[8,4,24,1280]{3,2,1,0:T(8,128)(2,1)}, bf16[8,4,24,1280]{3,2,1,0:T(8,128)(2,1)}) custom-call(bf16[128,1280]{1,0:T(8,128)(2,1)} %fusion.refs_0_, s32[1,128]{1,0:T(1,128)} %refs_1_.3, bf16[20,1280]{1,0:T(8,128)(2,1)} %bitcast.45, bf16[480,1280]{1,0:T(8,128)(2,1)} %bitcast.43), custom_call_target="tpu_custom_call" | custom-call | tf_op jit(solution)/shard_map/pallas_call | solution.py:284
  171.2 0.0 copy-start.1
  171.2 0.0 copy-start.3
  171.3 2.4 %fusion.17 = f32[768,128]{1,0:T(8,128)S(1)} fusion(bf16[768,1280]{1,0:T(8,128)(2,1)} %bitcast.33, bf16[1280,128]{1,0:T(8,128)(2,1)} %bitcast.38), kind=kOutput, calls=%fused_computation.45 | convolution fusion | flops 251658240 | bytes 2686976 | tf_op jit(solution)/shard_map/dot_general | solution.py:432
  173.6 0.0 copy-done.1
  173.7 0.0 copy-done.3
  173.7 0.7 broadcast_select_fusion.1
  174.3 0.0 copy-start
  174.4 0.1 copy_bitcast_fusion
  174.4 0.1 reshape.87
  174.5 0.2 copy.35
  174.7 0.6 copy-done
  175.3 0.8 add_convert_fusion
  (4 shorter events, 0.0 us)
Async XLA Ops:
  56.9 2.4 %copy-start.2 = (bf16[8,4,24,1280]{3,2,1,0:T(8,128)(2,1)S(1)}, bf16[8,4,24,1280]{3,2,1,0:T(8,128)(2,1)}, u32[]{:S(2)}) copy-start(bf16[8,4,24,1280]{3,2,1,0:T(8,128)(2,1)} %get-tuple-element.11) | copy-start | bytes 5898244
  56.9 2.4 %copy-start.4 = (bf16[8,160,128]{2,1,0:T(8,128)(2,1)S(1)}, bf16[8,160,128]{2,1,0:T(8,128)(2,1)}, u32[]{:S(2)}) copy-start(bf16[8,160,128]{2,1,0:T(8,128)(2,1)} %get-tuple-element.12) | copy-start | bytes 983044
  60.1 1.6 copy-start.6
  62.0 62.0 %copy-start.5 = (bf16[128,1280]{1,0:T(8,128)(2,1)S(1)}, bf16[128,1280]{1,0:T(8,128)(2,1)}, u32[]{:S(2)}) copy-start(bf16[128,1280]{1,0:T(8,128)(2,1)} %param.15) | copy-start | bytes 983044
  171.2 2.4 %copy-start.1 = (bf16[8,4,24,1280]{3,2,1,0:T(8,128)(2,1)S(1)}, bf16[8,4,24,1280]{3,2,1,0:T(8,128)(2,1)}, u32[]{:S(2)}) copy-start(bf16[8,4,24,1280]{3,2,1,0:T(8,128)(2,1)} %get-tuple-element.14) | copy-start | bytes 5898244
  171.2 2.4 %copy-start.3 = (bf16[8,160,128]{2,1,0:T(8,128)(2,1)S(1)}, bf16[8,160,128]{2,1,0:T(8,128)(2,1)}, u32[]{:S(2)}) copy-start(bf16[8,160,128]{2,1,0:T(8,128)(2,1)} %get-tuple-element.15) | copy-start | bytes 983044
  174.3 1.0 copy-start

commit v6 on v5

--- a/solution.py
+++ b/solution.py
@@ -225,7 +225,6 @@
         row_ring[way, 3, way].wait_recv()
     label_ring[0, 3].wait_recv()
     project(block_of(0, 4))
-    shard_step(4)
     def store(targets, here, mixed):
         for index, target in enumerate(targets):
             heads[target, here, :] = mixed[:, index * LANES : (index + 1) * LANES]
@@ -242,7 +241,9 @@
 
     keep_heads = pltpu.make_async_copy(heads.at[tp], received.at[tp], local_sem.at[2])
     label_rows = [labels[part].astype(jnp.float32) for part in range(N_TP)]
-    for targets in attend(qv, keys, label_rows, store, causal):
+    for done, targets in enumerate(attend(qv, keys, label_rows, store, causal)):
+        if done == 0:
+            shard_step(4)
         for target in targets:
 
             @pl.when(tp != target)

time: 177 us -> 177 us (level)
  blocking collectives: 18.8 us -> 20.6 us
    all_to_all x1, blocking collectives: 18.8 us -> 20.6 us  [per_device(): lax.all_to_all(send_rows, 'grp', split_axis=0, concat_axis=0, tiled=True)]
where the time goes in v6:
time: 177 us; the launch traced here: 176 us
  Pallas kernels  142 us (80%)
  blocking collectives  20.6 us (12%)
  matrix products  8.2 us (5%)
  local copies, waits for them, and re-layouts  3.61 us (2%)
  other arithmetic  1.79 us (1%)
    pallas_call x2, Pallas kernels, run_layer(): pl.pallas_call(functools.partial(layer_kernel, causal), out_shape=[jax.Sh...  101 us
    pallas_call x1, Pallas kernels, merge_rows(): pl.pallas_call(merge_kernel, out_shape=jax.ShapeDtypeStruct((row_total, N...  41.2 us
    all_to_all x1, blocking collectives, per_device(): lax.all_to_all(send_rows, 'grp', split_axis=0, concat_axis=0, tiled=True)  20.6 us
    dot_general x4, matrix products, project(): return jnp.dot(flat, own_heads, preferred_element_type=jnp.float32)  6.12 us

profile of v6, /device:TPU:56, one launch (start us, length us, event | category | flops | bytes accessed | tf_op | source)
XLA Modules:
  0.0 176.5 jit_solution(14492116610195454096)
XLA Ops:
  0.0 1.2 copy.29
  1.2 54.5 %shard_map.100 = (bf16[8,160,128]{2,1,0:T(8,128)(2,1)}, bf16[8,4,24,1280]{3,2,1,0:T(8,128)(2,1)}, bf16[8,4,24,1280]{3,2,1,0:T(8,128)(2,1)}) custom-call(bf16[128,1280]{1,0:T(8,128)(2,1)} %refs_0_.1, s32[1,128]{1,0:T(1,128)} %refs_1_.2, bf16[20,1280]{1,0:T(8,128)(2,1)} %bitcast.44, bf16[480,1280]{1,0:T(8,128)(2,1)} %bitcast.42), custom_call_target="tpu_custom_call" | custom-call | tf_op jit(solution)/shard_map/pallas_call | solution.py:285
  55.7 0.0 copy-start.2
  55.7 0.0 copy-start.4
  55.7 2.4 %fusion.16 = f32[768,128]{1,0:T(8,128)S(1)} fusion(bf16[768,1280]{1,0:T(8,128)(2,1)} %bitcast.32, bf16[1280,128]{1,0:T(8,128)(2,1)} %bitcast.40), kind=kOutput, calls=%fused_computation.44 | convolution fusion | flops 251658240 | bytes 2686976 | tf_op jit(solution)/shard_map/dot_general | solution.py:433
  58.1 0.0 copy-done.2
  58.1 0.0 copy-done.4
  58.1 0.7 broadcast_select_fusion.3
  58.8 0.1 copy_bitcast_fusion.1
  58.9 0.1 reshape.79
  58.9 0.0 copy-start.6
  59.0 0.2 convert_reduce_fusion
  59.2 0.2 fusion.3
  59.3 0.1 fusion.4
  59.4 0.2 copy.32
  59.6 0.9 reshape.80.own
  60.6 0.0 copy-done.6
  60.6 0.2 convert_reduce_fusion.1
  60.8 0.0 copy-start.5
  60.8 41.2 %shard_map.101 = bf16[32,1280]{1,0:T(8,128)(2,1)} custom-call(bf16[32,5120]{1,0:T(8,128)(2,1)} %reshape.80.own, bf16[160,5120]{1,0:T(8,128)(2,1)} %weights_hbm.1), custom_call_target="tpu_custom_call" | custom-call | tf_op jit(solution)/shard_map/pallas_call | solution.py:407
  102.0 0.1 broadcast_in_dim.7
  102.1 1.1 convolution_convert_fusion.1
  103.2 0.1 reshape.81
  103.4 20.6 %all_to_all.5 = bf16[64,2,1408]{2,1,0:T(2,128)(2,1)S(1)} all-to-all(bf16[64,2,1408]{2,1,0:T(2,128)(2,1)S(1)} %reshape.81), channel_id=1, replica_groups=mesh['grp'=64,'tp'=8] {'grp'}, dimensions={0} | all-to-all | bytes 720896 | tf_op jit(solution)/shard_map/all_to_all | solution.py:471
  124.0 0.1 reshape.82
  124.1 0.1 add_reduce_fusion
  124.3 0.1 fusion.9
  124.4 0.0 copy-done.5
  124.4 1.0 fusion.refs_0_
  125.4 46.2 %shard_map.102 = (bf16[8,160,128]{2,1,0:T(8,128)(2,1)}, bf16[8,4,24,1280]{3,2,1,0:T(8,128)(2,1)}, bf16[8,4,24,1280]{3,2,1,0:T(8,128)(2,1)}) custom-call(bf16[128,1280]{1,0:T(8,128)(2,1)} %fusion.refs_0_, s32[1,128]{1,0:T(1,128)} %refs_1_.3, bf16[20,1280]{1,0:T(8,128)(2,1)} %bitcast.45, bf16[480,1280]{1,0:T(8,128)(2,1)} %bitcast.43), custom_call_target="tpu_custom_call" | custom-call | tf_op jit(solution)/shard_map/pallas_call | solution.py:285
  171.6 0.0 copy-start.1
  171.6 0.0 copy-start.3
  171.6 2.4 %fusion.17 = f32[768,128]{1,0:T(8,128)S(1)} fusion(bf16[768,1280]{1,0:T(8,128)(2,1)} %bitcast.33, bf16[1280,128]{1,0:T(8,128)(2,1)} %bitcast.38), kind=kOutput, calls=%fused_computation.45 | convolution fusion | flops 251658240 | bytes 2686976 | tf_op jit(solution)/shard_map/dot_general | solution.py:433
  174.0 0.0 copy-done.1
  174.0 0.0 copy-done.3
  174.0 0.7 broadcast_select_fusion.1
  174.7 0.0 copy-start
  174.7 0.1 copy_bitcast_fusion
  174.8 0.1 reshape.87
  174.9 0.2 copy.35
  175.1 0.6 copy-done
  175.7 0.8 add_convert_fusion
  (4 shorter events, 0.0 us)
Async XLA Ops:
  55.7 2.4 %copy-start.2 = (bf16[8,4,24,1280]{3,2,1,0:T(8,128)(2,1)S(1)}, bf16[8,4,24,1280]{3,2,1,0:T(8,128)(2,1)}, u32[]{:S(2)}) copy-start(bf16[8,4,24,1280]{3,2,1,0:T(8,128)(2,1)} %get-tuple-element.11) | copy-start | bytes 5898244
  55.7 2.4 %copy-start.4 = (bf16[8,160,128]{2,1,0:T(8,128)(2,1)S(1)}, bf16[8,160,128]{2,1,0:T(8,128)(2,1)}, u32[]{:S(2)}) copy-start(bf16[8,160,128]{2,1,0:T(8,128)(2,1)} %get-tuple-element.12) | copy-start | bytes 983044
  58.9 1.6 copy-start.6
  60.8 63.6 %copy-start.5 = (bf16[128,1280]{1,0:T(8,128)(2,1)S(1)}, bf16[128,1280]{1,0:T(8,128)(2,1)}, u32[]{:S(2)}) copy-start(bf16[128,1280]{1,0:T(8,128)(2,1)} %param.15) | copy-start | bytes 983044
  171.6 2.4 %copy-start.1 = (bf16[8,4,24,1280]{3,2,1,0:T(8,128)(2,1)S(1)}, bf16[8,4,24,1280]{3,2,1,0:T(8,128)(2,1)}, u32[]{:S(2)}) copy-start(bf16[8,4,24,1280]{3,2,1,0:T(8,128)(2,1)} %get-tuple-element.14) | copy-start | bytes 5898244
  171.6 2.4 %copy-start.3 = (bf16[8,160,128]{2,1,0:T(8,128)(2,1)S(1)}, bf16[8,160,128]{2,1,0:T(8,128)(2,1)}, u32[]{:S(2)}) copy-start(bf16[8,160,128]{2,1,0:T(8,128)(2,1)} %get-tuple-element.15) | copy-start | bytes 983044
  174.7 1.0 copy-start
